TPU v7x, 32 devices: a whole 2x2x4 slice. The times are simulated.
32 devices in a mesh: grp: 2 (over x), ta: 4 (over y, core), gz: 4 (over z).
Axes of the slice: x: 2, y: 2, z: 4, core: 2. Of those that a mesh axis runs over, the one named last changes fastest.
Arguments:
- coarse_links: bfloat16 [4, 4, 16, 9, 128, 128], P('ta', 'gz'), may hold values from -5 to 5
- right_sides: float32 [16, 4, 4, 16, 128], P(None, 'ta', 'gz', 'grp'), may hold values from -12 to 12
Outputs:
- solution: float32 [16, 4, 4, 16, 128], P(None, 'ta', 'gz', 'grp')
- residual: float32 [16, 4, 4, 16, 128], P(None, 'ta', 'gz', 'grp')
All inputs are finite; a program needn't handle non-finite values.
Results may differ from a plain program's by a relative error of at most 0.015.
The roundings to bfloat16 on the way count: a program that leaves them out, or rounds other values in their place, can miss the bound.
Values may be sent and summed in bfloat16 or wider, within the bound.
No kernel may reach another device: no remote copies, remote signals or barrier semaphores. Data moves between devices by JAX's collectives and lax.ppermute only.
A program may use at most 64 MiB of HBM per device.

v0:
```python
import jax
import jax.numpy as jnp
import numpy as np
from jax import lax
from jax.sharding import PartitionSpec as P

LX = 4
LY = 4
ITERS = 4


def extended(block, sides, width):
    for axis, dim in sides:
        count = lax.axis_size(axis)
        forward = [(i, i + 1) for i in range(count - 1)]
        forward.append((count - 1, 0))
        backward = [(target, source) for source, target in forward]
        low = lax.ppermute(
            lax.slice_in_dim(block, block.shape[dim] - width, None, axis=dim), axis, forward
        )
        high = lax.ppermute(lax.slice_in_dim(block, 0, width, axis=dim), axis, backward)
        block = jnp.concatenate([low, block, high], axis=dim)
    return block


def site_table():
    site_ids = np.arange(LX * LY)
    column = site_ids % LX
    row_of = site_ids // LX
    forward_x = row_of * LX + (column + 1) % LX
    backward_x = row_of * LX + (column - 1) % LX
    forward_y = (row_of + 1) % LY * LX + column
    backward_y = (row_of - 1) % LY * LX + column
    return np.stack([forward_x, backward_x, forward_y, backward_y], axis=1).astype(np.int32)


def hopping(link_part, centre, xy_plane, padded, table_part):
    extent = centre.shape
    planar = jnp.take(xy_plane, table_part.reshape(-1), axis=3).reshape(extent[:4] + (4, extent[4]))
    upper_z = padded[:, 1:-1, 2:]
    lower_z = padded[:, 1:-1, :-2]
    upper_t = padded[:, 2:, 1:-1]
    lower_t = padded[:, :-2, 1:-1]
    stacked = jnp.concatenate(
        [
            centre[:, :, :, :, None, :],
            planar,
            upper_z[:, :, :, :, None, :],
            lower_z[:, :, :, :, None, :],
            upper_t[:, :, :, :, None, :],
            lower_t[:, :, :, :, None, :],
        ],
        axis=4,
    )
    return jnp.einsum(
        "tzsmab,rtzsmb->rtzsa", link_part, stacked, preferred_element_type=jnp.float32
    )


def inner(left, right):
    return jnp.sum(left * right, axis=(1, 2, 3, 4))


def expand(values):
    return values.reshape(-1, 1, 1, 1, 1)


def solve(right_sides, apply_op, coeff_total, norm_total):
    solution = jnp.zeros_like(right_sides)
    residual = right_sides
    basis_q = []
    basis_p = []
    for iteration in range(ITERS):
        direction = residual.astype(jnp.bfloat16)
        mapped = apply_op(direction)
        search = direction.astype(jnp.float32)
        previous = len(basis_q)
        if previous > 0:
            coefficients = coeff_total(
                jnp.stack([inner(older, mapped) for older in basis_q], axis=1)
            )
        ortho_q = mapped
        ortho_p = search
        for position in range(previous):
            ortho_q = ortho_q - expand(coefficients[:, position]) * basis_q[position]
            ortho_p = ortho_p - expand(coefficients[:, position]) * basis_p[position]
        totals = norm_total(jnp.stack([inner(ortho_q, ortho_q), inner(ortho_q, residual)], axis=1))
        squared = totals[:, 0]
        projected = totals[:, 1]
        inverse = 1.0 / jnp.sqrt(squared)
        new_q = ortho_q * expand(inverse)
        new_p = ortho_p * expand(inverse)
        alpha = projected * inverse
        solution = solution + expand(alpha) * new_p
        residual = residual - expand(alpha) * new_q
        basis_q.append(new_q)
        basis_p.append(new_p)
    return (solution, residual)


def local(coarse_links, right_sides):
    full_table = jnp.asarray(site_table())
    site_count = right_sides.shape[3]
    offset = lax.axis_index("grp") * site_count
    link_part = lax.dynamic_slice_in_dim(coarse_links, offset, site_count, 2)
    table_part = lax.dynamic_slice_in_dim(full_table, offset, site_count, 0)

    def operate_sites(direction):
        xy_plane = lax.all_gather(direction, "grp", axis=3, tiled=True)
        padded = extended(direction, (("ta", 1), ("gz", 2)), 1)
        return hopping(link_part, direction, xy_plane, padded, table_part)

    def coeff_sites(values):
        return lax.psum(values, ("grp", "ta", "gz"))

    def norm_sites(values):
        return lax.psum(values, ("grp", "ta", "gz"))

    solution, residual = solve(right_sides, operate_sites, coeff_sites, norm_sites)
    return (solution, residual)


def solution(mesh):
    placed = (P("ta", "gz", None, None, None, None), P(None, "ta", "gz", "grp", None))
    return jax.shard_map(
        local,
        mesh=mesh,
        in_specs=placed,
        out_specs=(P(None, "ta", "gz", "grp", None), P(None, "ta", "gz", "grp", None)),
        check_vma=False,
    )
```

profile of v0, /device:TPU:0, one launch (start us, length us, event | category | flops | bytes accessed | tf_op | source)
XLA Modules:
  0.0 355.1 jit_solution(9772201396584370104)
XLA Ops:
  0.6 0.9 constant_dynamic-update-slice_fusion.5
  1.5 2.5 collective-permute-start.1
  4.0 0.7 constant_dynamic-slice_fusion
  4.8 4.7 %all_gather.12 = bf16[16,1,1,16,128]{4,0,2,1,3:T(8,128)(2,1)S(1)} all-gather(bf16[16,1,1,8,128]{4,0,2,1,3:T(8,128)(2,1)S(1)} %bitcast.250), channel_id=1, replica_groups=mesh['grp'=2,'ta'=4,'gz'=4] {'grp'}, dimensions={3}, use_global_device_ids=true | all-gather | bytes 98304 | tf_op jit(solution)/shard_map/all_gather | solution.py:109
  10.2 3.7 %collective-permute-start.2 = (bf16[16,3,1,8,128]{4,0,3,2,1:T(8,128)(2,1)S(1)}, bf16[16,3,1,8,128]{4,0,3,2,1:T(8,128)(2,1)S(1)}, u32[]{:S(2)}, u32[]{:S(2)}) collective-permute-start(bf16[16,3,1,8,128]{4,0,3,2,1:T(8,128)(2,1)S(1)} %pad_maximum_fusion), channel_id=1, source_target_pairs={{1,0},{2,1},{3,2},{0,3},{5,4},{6,5},{7,6},{4,7},{9,8},{10,9},{11,1... | collective-permute-start | bytes 294920 | tf_op jit(solution)/shard_map/ppermute | solution.py:21
  14.0 3.1 collective-permute-done.2
  17.1 3.3 collective-permute-done.3
  20.4 2.6 multiply_reduce_fusion.13
  23.0 38.8 %psum.49 = f32[16,2]{0,1:T(2,128)S(1)} all-reduce(f32[16,2]{0,1:T(2,128)S(1)} %pad_maximum_fusion.5), channel_id=1, replica_groups=mesh['grp'=2,'ta'=4,'gz'=4] {'grp','ta','gz'}, use_global_device_ids=true, to_apply=%region_2.4 | all-reduce | flops 32 | bytes 256 | tf_op jit(solution)/shard_map/psum | solution.py:117
  61.8 0.9 constant_dynamic-update-slice_fusion.11
  63.3 4.8 %all_gather.13 = bf16[16,1,1,16,128]{4,0,2,1,3:T(8,128)(2,1)S(1)} all-gather(bf16[16,1,1,8,128]{4,0,2,1,3:T(8,128)(2,1)S(1)} %bitcast.251), channel_id=1, replica_groups=mesh['grp'=2,'ta'=4,'gz'=4] {'grp'}, dimensions={3}, use_global_device_ids=true | all-gather | bytes 98304 | tf_op jit(solution)/shard_map/all_gather | solution.py:109
  68.9 1.6 collective-permute-start.6
  71.0 3.1 collective-permute-done.6
  74.2 3.2 collective-permute-done.7
  77.4 2.6 multiply_reduce_fusion.11
  80.0 38.6 %psum.50 = f32[16]{0:T(128)S(1)} all-reduce(f32[16]{0:T(128)S(1)} %get-tuple-element.42), channel_id=1, replica_groups=mesh['grp'=2,'ta'=4,'gz'=4] {'grp','ta','gz'}, use_global_device_ids=true, to_apply=%region_4.6 | all-reduce | flops 16 | bytes 128 | tf_op jit(solution)/shard_map/psum | solution.py:114
  118.8 40.8 %psum.51 = f32[16,2]{0,1:T(2,128)S(1)} all-reduce(f32[16,2]{0,1:T(2,128)S(1)} %pad_maximum_fusion.6), channel_id=1, replica_groups=mesh['grp'=2,'ta'=4,'gz'=4] {'grp','ta','gz'}, use_global_device_ids=true, to_apply=%region_7.9 | all-reduce | flops 32 | bytes 256 | tf_op jit(solution)/shard_map/psum | solution.py:117
  160.2 4.8 %all_gather.14 = bf16[16,1,1,16,128]{4,0,2,1,3:T(8,128)(2,1)S(1)} all-gather(bf16[16,1,1,8,128]{4,0,2,1,3:T(8,128)(2,1)S(1)} %bitcast.252), channel_id=1, replica_groups=mesh['grp'=2,'ta'=4,'gz'=4] {'grp'}, dimensions={3}, use_global_device_ids=true | all-gather | bytes 98304 | tf_op jit(solution)/shard_map/all_gather | solution.py:109
  165.8 1.6 collective-permute-start.10
  167.9 3.1 collective-permute-done.10
  171.1 3.1 collective-permute-done.11
  174.2 2.6 multiply_reduce_fusion.8
  176.8 38.2 %psum.52 = f32[16,2]{0,1:T(2,128)S(1)} all-reduce(f32[16,2]{0,1:T(2,128)S(1)} %pad_maximum_fusion.7), channel_id=1, replica_groups=mesh['grp'=2,'ta'=4,'gz'=4] {'grp','ta','gz'}, use_global_device_ids=true, to_apply=%region_10.12 | all-reduce | flops 32 | bytes 256 | tf_op jit(solution)/shard_map/psum | solution.py:114
  215.3 41.4 %psum.53 = f32[16,2]{0,1:T(2,128)S(1)} all-reduce(f32[16,2]{0,1:T(2,128)S(1)} %pad_maximum_fusion.8), channel_id=1, replica_groups=mesh['grp'=2,'ta'=4,'gz'=4] {'grp','ta','gz'}, use_global_device_ids=true, to_apply=%region_13.15 | all-reduce | flops 32 | bytes 256 | tf_op jit(solution)/shard_map/psum | solution.py:117
  257.4 4.8 %all_gather.15 = bf16[16,1,1,16,128]{4,0,2,1,3:T(8,128)(2,1)S(1)} all-gather(bf16[16,1,1,8,128]{4,0,2,1,3:T(8,128)(2,1)S(1)} %bitcast.253), channel_id=1, replica_groups=mesh['grp'=2,'ta'=4,'gz'=4] {'grp'}, dimensions={3}, use_global_device_ids=true | all-gather | bytes 98304 | tf_op jit(solution)/shard_map/all_gather | solution.py:109
  263.0 1.6 collective-permute-start.14
  265.1 3.1 collective-permute-done.14
  268.3 3.1 collective-permute-done.15
  271.4 2.6 multiply_reduce_fusion.4
  274.0 38.7 %psum.54 = f32[16,3]{0,1:T(4,128)S(1)} all-reduce(f32[16,3]{0,1:T(4,128)S(1)} %pad_maximum_fusion.4), channel_id=1, replica_groups=mesh['grp'=2,'ta'=4,'gz'=4] {'grp','ta','gz'}, use_global_device_ids=true, to_apply=%region_17.19 | all-reduce | flops 48 | bytes 384 | tf_op jit(solution)/shard_map/psum | solution.py:114
  313.0 40.6 %psum.55 = f32[16,2]{0,1:T(2,128)S(1)} all-reduce(f32[16,2]{0,1:T(2,128)S(1)} %pad_maximum_fusion.9), channel_id=1, replica_groups=mesh['grp'=2,'ta'=4,'gz'=4] {'grp','ta','gz'}, use_global_device_ids=true, to_apply=%region_20.22 | all-reduce | flops 32 | bytes 256 | tf_op jit(solution)/shard_map/psum | solution.py:117
  353.8 0.7 copy.80
  (79 shorter events, 8.3 us)
Async XLA Ops:
  1.5 8.7 %collective-permute-start.1 = (bf16[16,1,1,8,128]{4,0,3,2,1:T(8,128)(2,1)S(1)}, bf16[16,1,1,8,128]{4,0,3,2,1:T(8,128)(2,1)S(1)}, u32[]{:S(2)}, u32[]{:S(2)}) collective-permute-start(bf16[16,1,1,8,128]{4,0,3,2,1:T(8,128)(2,1)S(1)} %get-tuple-element.35), channel_id=1, source_target_pairs={{4,0},{8,4},{12,8},{0,12},{5,1},{9,5},{13,9},{1,13},{6,2},{10,6},{... | collective-permute-start | bytes 98312 | tf_op jit(solution)/shard_map/ppermute | solution.py:21
  4.0 6.2 %collective-permute-start = (bf16[16,1,1,8,128]{4,0,3,2,1:T(8,128)(2,1)S(1)}, bf16[16,1,1,8,128]{4,0,3,2,1:T(8,128)(2,1)S(1)}, u32[]{:S(2)}, u32[]{:S(2)}) collective-permute-start(bf16[16,1,1,8,128]{4,0,3,2,1:T(8,128)(2,1)S(1)} %get-tuple-element.35), channel_id=1, source_target_pairs={{0,4},{4,8},{8,12},{12,0},{1,5},{5,9},{9,13},{13,1},{2,6},{6,10},{... | collective-permute-start | bytes 98312 | tf_op jit(solution)/shard_map/ppermute | solution.py:18
  10.2 6.8 %collective-permute-start.2 = (bf16[16,3,1,8,128]{4,0,3,2,1:T(8,128)(2,1)S(1)}, bf16[16,3,1,8,128]{4,0,3,2,1:T(8,128)(2,1)S(1)}, u32[]{:S(2)}, u32[]{:S(2)}) collective-permute-start(bf16[16,3,1,8,128]{4,0,3,2,1:T(8,128)(2,1)S(1)} %pad_maximum_fusion), channel_id=1, source_target_pairs={{1,0},{2,1},{3,2},{0,3},{5,4},{6,5},{7,6},{4,7},{9,8},{10,9},{11,1... | collective-permute-start | bytes 294920 | tf_op jit(solution)/shard_map/ppermute | solution.py:21
  13.9 6.5 %collective-permute-start.3 = (bf16[16,3,1,8,128]{4,0,3,2,1:T(8,128)(2,1)S(1)}, bf16[16,3,1,8,128]{4,0,3,2,1:T(8,128)(2,1)S(1)}, u32[]{:S(2)}, u32[]{:S(2)}) collective-permute-start(bf16[16,3,1,8,128]{4,0,3,2,1:T(8,128)(2,1)S(1)} %pad_maximum_fusion), channel_id=1, source_target_pairs={{0,1},{1,2},{2,3},{3,0},{4,5},{5,6},{6,7},{7,4},{8,9},{9,10},{10,1... | collective-permute-start | bytes 294920 | tf_op jit(solution)/shard_map/ppermute | solution.py:18
  62.8 6.1 %collective-permute-start.5 = (bf16[16,1,1,8,128]{4,0,3,2,1:T(8,128)(2,1)S(1)}, bf16[16,1,1,8,128]{4,0,3,2,1:T(8,128)(2,1)S(1)}, u32[]{:S(2)}, u32[]{:S(2)}) collective-permute-start(bf16[16,1,1,8,128]{4,0,3,2,1:T(8,128)(2,1)S(1)} %get-tuple-element.32), channel_id=1, source_target_pairs={{4,0},{8,4},{12,8},{0,12},{5,1},{9,5},{13,9},{1,13},{6,2},{10,6},{... | collective-permute-start | bytes 98312 | tf_op jit(solution)/shard_map/ppermute | solution.py:21
  62.9 6.0 %collective-permute-start.4 = (bf16[16,1,1,8,128]{4,0,3,2,1:T(8,128)(2,1)S(1)}, bf16[16,1,1,8,128]{4,0,3,2,1:T(8,128)(2,1)S(1)}, u32[]{:S(2)}, u32[]{:S(2)}) collective-permute-start(bf16[16,1,1,8,128]{4,0,3,2,1:T(8,128)(2,1)S(1)} %get-tuple-element.32), channel_id=1, source_target_pairs={{0,4},{4,8},{8,12},{12,0},{1,5},{5,9},{9,13},{13,1},{2,6},{6,10},{... | collective-permute-start | bytes 98312 | tf_op jit(solution)/shard_map/ppermute | solution.py:18
  68.9 5.3 %collective-permute-start.6 = (bf16[16,3,1,8,128]{4,0,3,2,1:T(8,128)(2,1)S(1)}, bf16[16,3,1,8,128]{4,0,3,2,1:T(8,128)(2,1)S(1)}, u32[]{:S(2)}, u32[]{:S(2)}) collective-permute-start(bf16[16,3,1,8,128]{4,0,3,2,1:T(8,128)(2,1)S(1)} %pad_maximum_fusion.1), channel_id=1, source_target_pairs={{1,0},{2,1},{3,2},{0,3},{5,4},{6,5},{7,6},{4,7},{9,8},{10,9},{11,1... | collective-permute-start | bytes 294920 | tf_op jit(solution)/shard_map/ppermute | solution.py:21
  70.6 6.8 %collective-permute-start.7 = (bf16[16,3,1,8,128]{4,0,3,2,1:T(8,128)(2,1)S(1)}, bf16[16,3,1,8,128]{4,0,3,2,1:T(8,128)(2,1)S(1)}, u32[]{:S(2)}, u32[]{:S(2)}) collective-permute-start(bf16[16,3,1,8,128]{4,0,3,2,1:T(8,128)(2,1)S(1)} %pad_maximum_fusion.1), channel_id=1, source_target_pairs={{0,1},{1,2},{2,3},{3,0},{4,5},{5,6},{6,7},{7,4},{8,9},{9,10},{10,1... | collective-permute-start | bytes 294920 | tf_op jit(solution)/shard_map/ppermute | solution.py:18
  159.7 6.1 %collective-permute-start.9 = (bf16[16,1,1,8,128]{4,0,3,2,1:T(8,128)(2,1)S(1)}, bf16[16,1,1,8,128]{4,0,3,2,1:T(8,128)(2,1)S(1)}, u32[]{:S(2)}, u32[]{:S(2)}) collective-permute-start(bf16[16,1,1,8,128]{4,0,3,2,1:T(8,128)(2,1)S(1)} %get-tuple-element.28), channel_id=1, source_target_pairs={{4,0},{8,4},{12,8},{0,12},{5,1},{9,5},{13,9},{1,13},{6,2},{10,6},{... | collective-permute-start | bytes 98312 | tf_op jit(solution)/shard_map/ppermute | solution.py:21
  160.0 5.8 %collective-permute-start.8 = (bf16[16,1,1,8,128]{4,0,3,2,1:T(8,128)(2,1)S(1)}, bf16[16,1,1,8,128]{4,0,3,2,1:T(8,128)(2,1)S(1)}, u32[]{:S(2)}, u32[]{:S(2)}) collective-permute-start(bf16[16,1,1,8,128]{4,0,3,2,1:T(8,128)(2,1)S(1)} %get-tuple-element.28), channel_id=1, source_target_pairs={{0,4},{4,8},{8,12},{12,0},{1,5},{5,9},{9,13},{13,1},{2,6},{6,10},{... | collective-permute-start | bytes 98312 | tf_op jit(solution)/shard_map/ppermute | solution.py:18
  165.8 5.3 %collective-permute-start.10 = (bf16[16,3,1,8,128]{4,0,3,2,1:T(8,128)(2,1)S(1)}, bf16[16,3,1,8,128]{4,0,3,2,1:T(8,128)(2,1)S(1)}, u32[]{:S(2)}, u32[]{:S(2)}) collective-permute-start(bf16[16,3,1,8,128]{4,0,3,2,1:T(8,128)(2,1)S(1)} %pad_maximum_fusion.2), channel_id=1, source_target_pairs={{1,0},{2,1},{3,2},{0,3},{5,4},{6,5},{7,6},{4,7},{9,8},{10,9},{11,1... | collective-permute-start | bytes 294920 | tf_op jit(solution)/shard_map/ppermute | solution.py:21
  167.4 6.8 %collective-permute-start.11 = (bf16[16,3,1,8,128]{4,0,3,2,1:T(8,128)(2,1)S(1)}, bf16[16,3,1,8,128]{4,0,3,2,1:T(8,128)(2,1)S(1)}, u32[]{:S(2)}, u32[]{:S(2)}) collective-permute-start(bf16[16,3,1,8,128]{4,0,3,2,1:T(8,128)(2,1)S(1)} %pad_maximum_fusion.2), channel_id=1, source_target_pairs={{0,1},{1,2},{2,3},{3,0},{4,5},{5,6},{6,7},{7,4},{8,9},{9,10},{10,1... | collective-permute-start | bytes 294920 | tf_op jit(solution)/shard_map/ppermute | solution.py:18
  256.8 6.1 %collective-permute-start.13 = (bf16[16,1,1,8,128]{4,0,3,2,1:T(8,128)(2,1)S(1)}, bf16[16,1,1,8,128]{4,0,3,2,1:T(8,128)(2,1)S(1)}, u32[]{:S(2)}, u32[]{:S(2)}) collective-permute-start(bf16[16,1,1,8,128]{4,0,3,2,1:T(8,128)(2,1)S(1)} %get-tuple-element.24), channel_id=1, source_target_pairs={{4,0},{8,4},{12,8},{0,12},{5,1},{9,5},{13,9},{1,13},{6,2},{10,6},{... | collective-permute-start | bytes 98312 | tf_op jit(solution)/shard_map/ppermute | solution.py:21
  257.1 5.8 %collective-permute-start.12 = (bf16[16,1,1,8,128]{4,0,3,2,1:T(8,128)(2,1)S(1)}, bf16[16,1,1,8,128]{4,0,3,2,1:T(8,128)(2,1)S(1)}, u32[]{:S(2)}, u32[]{:S(2)}) collective-permute-start(bf16[16,1,1,8,128]{4,0,3,2,1:T(8,128)(2,1)S(1)} %get-tuple-element.24), channel_id=1, source_target_pairs={{0,4},{4,8},{8,12},{12,0},{1,5},{5,9},{9,13},{13,1},{2,6},{6,10},{... | collective-permute-start | bytes 98312 | tf_op jit(solution)/shard_map/ppermute | solution.py:18
  263.0 5.3 %collective-permute-start.14 = (bf16[16,3,1,8,128]{4,0,3,2,1:T(8,128)(2,1)S(1)}, bf16[16,3,1,8,128]{4,0,3,2,1:T(8,128)(2,1)S(1)}, u32[]{:S(2)}, u32[]{:S(2)}) collective-permute-start(bf16[16,3,1,8,128]{4,0,3,2,1:T(8,128)(2,1)S(1)} %pad_maximum_fusion.3), channel_id=1, source_target_pairs={{1,0},{2,1},{3,2},{0,3},{5,4},{6,5},{7,6},{4,7},{9,8},{10,9},{11,1... | collective-permute-start | bytes 294920 | tf_op jit(solution)/shard_map/ppermute | solution.py:21
  264.5 6.8 %collective-permute-start.15 = (bf16[16,3,1,8,128]{4,0,3,2,1:T(8,128)(2,1)S(1)}, bf16[16,3,1,8,128]{4,0,3,2,1:T(8,128)(2,1)S(1)}, u32[]{:S(2)}, u32[]{:S(2)}) collective-permute-start(bf16[16,3,1,8,128]{4,0,3,2,1:T(8,128)(2,1)S(1)} %pad_maximum_fusion.3), channel_id=1, source_target_pairs={{0,1},{1,2},{2,3},{3,0},{4,5},{5,6},{6,7},{7,4},{8,9},{9,10},{10,1... | collective-permute-start | bytes 294920 | tf_op jit(solution)/shard_map/ppermute | solution.py:18
where the time goes:
time: 356 us; the launch traced here: 355 us
  blocking collectives  296 us (83%)
  waiting for transfers between devices  25.2 us (7%)
  starting transfers between devices  14.3 us (4%)
  matrix products  10.3 us (3%)
  local copies, waits for them, and re-layouts  5.53 us (2%)
    psum x4, blocking collectives, norm_sites(): return lax.psum(values, ('grp', 'ta', 'gz'))  162 us
    psum x3, blocking collectives, coeff_sites(): return lax.psum(values, ('grp', 'ta', 'gz'))  116 us
    all_gather x4, blocking collectives, operate_sites(): xy_plane = lax.all_gather(direction, 'grp', axis=3, tiled=True)  19.1 us
    ppermute x8, waiting for transfers between devices, extended(): lax.ppermute(lax.slice_in_dim(block, block.shape[dim] - width, None, axis...  12.7 us
    ppermute x8, waiting for transfers between devices, extended(): lax.ppermute(lax.slice_in_dim(block, 0, width, axis=dim), axis, backward)  12.6 us
    ppermute x8, starting transfers between devices, extended(): lax.ppermute(lax.slice_in_dim(block, 0, width, axis=dim), axis, backward)  11.6 us
    dot_general x4, matrix products, hopping(): jnp.einsum('tzsmab,rtzsmb->rtzsa', link_part, stacked, preferred_element_...  10.3 us
  transfers between devices with their start and end apart: 16, of which 8 were waited for; matrix products, arithmetic and copies ran while one was open for 1% of the time, Pallas kernels for 0%

commit v1 on v0

v1 whole, which is shorter than its diff:
```python
import functools

import jax
import jax.numpy as jnp
import numpy as np
from jax import lax
from jax.experimental import pallas as pl
from jax.experimental.pallas import tpu as pltpu
from jax.sharding import PartitionSpec as P

LX = 4
LY = 4
ITERS = 4
AXES = ("grp", "ta", "gz")
LANES = 128


def site_table():
    site_ids = np.arange(LX * LY)
    column = site_ids % LX
    row_of = site_ids // LX
    forward_x = row_of * LX + (column + 1) % LX
    backward_x = row_of * LX + (column - 1) % LX
    forward_y = (row_of + 1) % LY * LX + column
    backward_y = (row_of - 1) % LY * LX + column
    return np.stack([forward_x, backward_x, forward_y, backward_y], axis=1).astype(np.int32)


def pairings(count):
    if count % 2 == 0:
        first = [(i, i ^ 1) for i in range(count)]
        second = [(i, (i + 1) % count if i % 2 else (i - 1) % count) for i in range(count)]
        return first, second, True
    up = [((i + 1) % count, i) for i in range(count)]
    return up, [(target, source) for source, target in up], False


def exchange(block):
    count = lax.axis_size("grp")
    blocks = []
    for shift in range(1, count):
        blocks.append(lax.ppermute(block, "grp", [((i + shift) % count, i) for i in range(count)]))
    for axis in ("ta", "gz"):
        first, second, _ = pairings(lax.axis_size(axis))
        blocks += [lax.ppermute(block, axis, first), lax.ppermute(block, axis, second)]
    return blocks


def arranged_links(coarse_links, site_count):
    offset = lax.axis_index("grp") * site_count
    part = lax.dynamic_slice_in_dim(coarse_links[0, 0], offset, site_count, 0)
    pieces = [part[:, :5]]
    for axis, base in (("ta", 7), ("gz", 5)):
        if pairings(lax.axis_size(axis))[2]:
            odd = lax.axis_index(axis) % 2
            pieces.append(lax.dynamic_slice_in_dim(part, base + odd, 1, 1))
            pieces.append(lax.dynamic_slice_in_dim(part, base + 1 - odd, 1, 1))
        else:
            pieces.append(part[:, base : base + 2])
    ordered = jnp.concatenate(pieces, axis=1)
    return jnp.swapaxes(ordered, 2, 3).reshape(site_count, -1, ordered.shape[2])


def columns(gathered, count, rhs):
    total = jnp.sum(gathered, axis=0, keepdims=True)
    spread = jnp.broadcast_to(total, (rhs, total.shape[1]))
    lane = lax.broadcasted_iota(jnp.int32, spread.shape, 1)
    row = lax.broadcasted_iota(jnp.int32, spread.shape, 0)
    return [
        jnp.sum(jnp.where(lane == row + index * rhs, spread, 0.0), axis=1, keepdims=True)
        for index in range(count)
    ]


def weights(gathered, previous, rhs):
    values = columns(gathered, previous + 2, rhs)
    coefficients = values[:previous]
    squared, projected = values[previous], values[previous + 1]
    for value in coefficients:
        squared = squared - value * value
    inverse = 1.0 / jnp.sqrt(squared)
    return coefficients, inverse, projected * inverse


def products(rows, links_ref, table_ref, plane_ref, blocks):
    plane = [value for block in blocks[: rows["plane"]] for value in block]
    neighbours = rows["neighbours"]
    if neighbours is None:
        for index, value in enumerate(plane):
            plane_ref[index] = value
    result = []
    for site in range(rows["sites"]):
        parts = [blocks[0][site]]
        if neighbours is None:
            parts += [plane_ref[table_ref[site, hop]] for hop in range(4)]
        else:
            parts += [plane[index] for index in neighbours[site]]
        parts += [block[site] for block in blocks[rows["plane"] :]]
        result.append(
            jnp.dot(
                jnp.concatenate(parts, axis=1),
                links_ref[site],
                preferred_element_type=jnp.float32,
            )
        )
    return result


def inner_rows(pairs, out_ref):
    stacked = []
    for left, right in pairs:
        total = left[0] * right[0]
        for a, b in zip(left[1:], right[1:]):
            total = total + a * b
        stacked.append(total)
    height = sum(value.shape[0] for value in stacked)
    if out_ref.shape[1] > height:
        stacked.append(jnp.zeros((out_ref.shape[1] - height, stacked[0].shape[1]), jnp.float32))
    table = jnp.concatenate(stacked, axis=0)
    ones = jnp.ones((out_ref.shape[0], table.shape[1]), jnp.float32)
    out_ref[...] = lax.dot_general(
        ones,
        table,
        (((1,), (1,)), ((), ())),
        precision=lax.Precision.HIGHEST,
        preferred_element_type=jnp.float32,
    )


def first_kernel(rows, table_ref, links_ref, *refs):
    count = rows["blocks"]
    residual_refs, (mapped_ref, dots_ref, plane_ref) = refs[:count], refs[count:]
    sites = range(rows["sites"])
    blocks = [[ref[site].astype(jnp.bfloat16) for site in sites] for ref in residual_refs]
    mapped = products(rows, links_ref, table_ref, plane_ref, blocks)
    own = [residual_refs[0][site] for site in sites]
    for site in sites:
        mapped_ref[site] = mapped[site]
    inner_rows([(mapped, mapped), (mapped, own)], dots_ref)


def next_kernel(rows, previous, table_ref, links_ref, gathered_ref, *refs):
    count = rows["blocks"]
    sites = range(rows["sites"])
    refs = list(refs)
    mapped_in, refs = refs[:count], refs[count:]
    if previous == 0:
        residual_in, refs = refs[:count], refs[count:]
    else:
        residual_in, refs = [refs[0].at[index] for index in range(count)], refs[1:]
    basis, refs = refs[:previous], refs[previous:]
    mapped_ref, dots_ref, residual_ref, new_ref, plane_ref = refs
    rhs = mapped_in[0].shape[1]
    coefficients, inverse, alpha = weights(gathered_ref[...], previous, rhs)
    blocks = []
    own = []
    for index in range(count):
        block = []
        for site in sites:
            q = mapped_in[index][site]
            for weight, older in zip(coefficients, basis):
                q = q - weight * older[index, site]
            q = q * inverse
            new_ref[index, site] = q
            residual = residual_in[index][site] - alpha * q
            residual_ref[index, site] = residual
            block.append(residual.astype(jnp.bfloat16))
            if index == 0:
                own.append(residual)
        blocks.append(block)
    mapped = products(rows, links_ref, table_ref, plane_ref, blocks)
    for site in sites:
        mapped_ref[site] = mapped[site]
    pairs = [
        ([older[0, site] for site in sites], mapped) for older in list(basis) + [new_ref]
    ]
    inner_rows(pairs + [(mapped, mapped), (mapped, own)], dots_ref)


def last_kernel(rows, last, *refs):
    refs = list(refs)
    gathered = refs[: last + 1]
    mapped_ref = refs[last + 1]
    residuals = refs[last + 2 : 2 * last + 3]
    basis = refs[2 * last + 3 : 3 * last + 3]
    solution_ref, residual_ref = refs[3 * last + 3 :]
    rhs = mapped_ref.shape[1]
    steps = [weights(ref[...], index, rhs) for index, ref in enumerate(gathered)]
    coefficients, inverse, alpha = steps[last]
    for site in range(rows["sites"]):
        q = mapped_ref[site]
        for weight, older in zip(coefficients, basis):
            q = q - weight * older[0, site]
        q = q * inverse
        current = [residuals[0][site]] + [ref[0, site] for ref in residuals[1:]]
        residual_ref[:, site, :] = current[last] - alpha * q
        found = []
        solution = None
        for index in range(last + 1):
            p = current[index].astype(jnp.bfloat16).astype(jnp.float32)
            for weight, older in zip(steps[index][0], found):
                p = p - weight * older
            p = p * steps[index][1]
            found.append(p)
            term = steps[index][2] * p
            solution = term if solution is None else solution + term
        solution_ref[:, site, :] = solution


def call(body, outs, operands, flops, table=None, scratch=()):
    vmem = pl.BlockSpec(memory_space=pltpu.VMEM)
    specs = [vmem] * len(operands)
    if table is not None:
        specs = [pl.BlockSpec(memory_space=pltpu.SMEM)] + specs
        operands = [table] + list(operands)
    size = sum(int(np.prod(v.shape)) * v.dtype.itemsize for v in list(outs) + list(operands))
    return pl.pallas_call(
        body,
        out_shape=tuple(outs),
        in_specs=specs,
        out_specs=tuple([vmem] * len(outs)),
        scratch_shapes=list(scratch),
        compiler_params=pltpu.CompilerParams(vmem_limit_bytes=16 * 1024 * 1024),
        cost_estimate=pl.CostEstimate(flops=flops, bytes_accessed=size, transcendentals=0),
    )(*operands)


def gather_all(dots):
    return lax.all_to_all(dots, AXES, 0, 0, tiled=True)


def local(coarse_links, right_sides):
    f32 = jnp.float32
    rhs, _, _, site_count, width = right_sides.shape
    group = lax.axis_size("grp")
    devices = group * lax.axis_size("ta") * lax.axis_size("gz")
    own = jnp.swapaxes(right_sides[:, 0, 0], 0, 1)
    table = site_table()
    rows = {"plane": group, "sites": site_count, "blocks": group + 4, "neighbours": None}
    dynamic = None
    scratch = [pltpu.VMEM((group * site_count, rhs, width), jnp.bfloat16)]
    if site_count % LX == 0:
        rows["neighbours"] = table[:site_count].tolist()
    else:
        offset = lax.axis_index("grp") * site_count
        places = lax.dynamic_slice_in_dim(jnp.asarray(table), offset, site_count, 0)
        dynamic = (places - offset + table.shape[0]) % table.shape[0]
    residual = [own] + exchange(own)
    links = arranged_links(coarse_links, site_count)
    flops = 2 * int(np.prod(links.shape)) * rhs
    slab = (rows["blocks"], site_count, rhs, width)

    def entry(body, *settings):
        settings = settings if dynamic is not None else settings + (None,)
        return functools.partial(body, *settings)

    def dots_shape(count):
        return jax.ShapeDtypeStruct((devices, -(-count * rhs // LANES) * LANES), f32)

    field = jax.ShapeDtypeStruct((site_count, rhs, width), f32)
    mapped, dots = call(
        entry(first_kernel, rows),
        [field, dots_shape(2)],
        [links] + residual,
        flops,
        dynamic,
        scratch,
    )
    gathered = []
    own_residuals = [own]
    basis = []
    for previous in range(ITERS - 1):
        gathered.append(gather_all(dots))
        halo = exchange(mapped)
        full = jax.ShapeDtypeStruct(slab, f32)
        mapped, dots, stacked, new = call(
            entry(next_kernel, rows, previous),
            [field, dots_shape(previous + 3), full, full],
            [links, gathered[-1], mapped] + halo + residual + basis,
            flops,
            dynamic,
            scratch,
        )
        residual = [stacked]
        own_residuals.append(stacked)
        basis.append(new)
    gathered.append(gather_all(dots))
    out = jax.ShapeDtypeStruct((rhs, site_count, width), f32)
    found, left = call(
        functools.partial(last_kernel, rows, ITERS - 1),
        [out, out],
        gathered + [mapped] + own_residuals + basis,
        flops // 100,
    )
    return (found.reshape(right_sides.shape), left.reshape(right_sides.shape))


def solution(mesh):
    placed = (P("ta", "gz", None, None, None, None), P(None, "ta", "gz", "grp", None))
    return jax.shard_map(
        local,
        mesh=mesh,
        in_specs=placed,
        out_specs=(P(None, "ta", "gz", "grp", None), P(None, "ta", "gz", "grp", None)),
        check_vma=False,
    )
```

time: 356 us -> 78.5 us (0.22)
  blocking collectives: 296 us -> 45.8 us
  waiting for transfers between devices: 25.2 us -> 0.05 us
  matrix products: 10.3 us -> 0 us
  local copies, waits for them, and re-layouts: 5.53 us -> 11.2 us
  Pallas kernels: 0 us -> 3.78 us
    psum x7 -> x0, blocking collectives: 277 us -> none  [the longest x4 162 us: norm_sites(): return lax.psum(values, ('grp', 'ta', 'gz'))]
    all_to_all x0 -> x4, blocking collectives: none -> 45.8 us  [gather_all(): return lax.all_to_all(dots, AXES, 0, 0, tiled=True)]
    ppermute x16 -> x20, waiting for transfers between devices: 25.2 us -> 0.05 us  [the longest x8 0.02 us: exchange(): lax.ppermute(block, axis, first)]
    all_gather x4 -> x0, blocking collectives: 19.1 us -> none  [operate_sites(): xy_plane = lax.all_gather(direction, 'grp', axis=3, tiled=True)]
    dot_general x4 -> x0, matrix products: 10.3 us -> none  [hopping(): jnp.einsum('tzsmab,rtzsmb->rtzsa', link_part, stacked, preferred_element_...]
    pallas_call x0 -> x5, Pallas kernels: none -> 3.78 us  [call(): pl.pallas_call(body, out_shape=tuple(outs), in_specs=specs, out_specs=tup...]
    ppermute x16 -> x20, starting transfers between devices: 14.3 us -> 16.4 us  [the longest x8 7.94 us: exchange(): lax.ppermute(block, axis, second)]
  transfers between devices with their start and end apart: 16 -> 20, of which waited for: 8 -> 0; matrix products, arithmetic and copies ran while one was open for 1% -> 11% of each run, Pallas kernels for 0% -> 0%
where the time goes in v1:
time: 78.5 us; the launch traced here: 78.1 us
  blocking collectives  45.8 us (58%)
  starting transfers between devices  16.4 us (21%)
  local copies, waits for them, and re-layouts  11.2 us (14%)
  Pallas kernels  3.78 us (5%)
  between operations  0.79 us (1%)
    all_to_all x4, blocking collectives, gather_all(): return lax.all_to_all(dots, AXES, 0, 0, tiled=True)  45.8 us
    ppermute x8, starting transfers between devices, exchange(): lax.ppermute(block, axis, second)  7.94 us
    unnamed x7, local copies, waits for them, and re-layouts  5.36 us
    ppermute x8, starting transfers between devices, exchange(): lax.ppermute(block, axis, first)  5.21 us
    pallas_call x5, Pallas kernels, call(): pl.pallas_call(body, out_shape=tuple(outs), in_specs=specs, out_specs=tup...  3.78 us
    ppermute x4, starting transfers between devices, exchange(): lax.ppermute(block, 'grp', [((i + shift) % count, i) for i in range(count)])  3.21 us
    transpose x1, local copies, waits for them, and re-layouts, arranged_links(): return jnp.swapaxes(ordered, 2, 3).reshape(site_count, -1, ordered.shape[2])  3.05 us
    dynamic_slice x1, local copies, waits for them, and re-layouts, arranged_links(): part = lax.dynamic_slice_in_dim(coarse_links[0, 0], offset, site_count, 0)  1.82 us
  transfers between devices with their start and end apart: 20, of which 0 were waited for; matrix products, arithmetic and copies ran while one was open for 11% of the time, Pallas kernels for 0%

profile of v1, /device:TPU:0, one launch (start us, length us, event | category | flops | bytes accessed | tf_op | source)
XLA Modules:
  0.0 78.1 jit_solution(523180927117797533)
XLA Ops:
  0.6 0.9 %copy.40 = f32[16,1,1,8,128]{4,0,3,2,1:T(8,128)S(1)} copy(f32[16,1,1,8,128]{4,3,2,1,0:T(8,128)} %param.3) | data formatting | bytes 131072 | tf_op args[1]
  1.5 5.1 %collective-permute-start.4 = (f32[8,16,128]{2,1,0:T(8,128)S(1)}, f32[8,16,128]{2,1,0:T(8,128)S(1)}, u32[]{:S(2)}, u32[]{:S(2)}) collective-permute-start(f32[8,16,128]{2,1,0:T(8,128)S(1)} %bitcast.59), channel_id=1, source_target_pairs={{0,3},{1,2},{2,1},{3,0},{4,7},{5,6},{6,5},{7,4},{8,11},{9,10},{10,... | collective-permute-start | bytes 196616 | tf_op jit(solution)/shard_map/ppermute | solution.py:45
  6.6 0.7 collective-permute-start.2
  7.3 1.0 %collective-permute-start.1 = (f32[8,16,128]{2,1,0:T(8,128)S(1)}, f32[8,16,128]{2,1,0:T(8,128)S(1)}, u32[]{:S(2)}, u32[]{:S(2)}) collective-permute-start(f32[8,16,128]{2,1,0:T(8,128)S(1)} %bitcast.62), channel_id=1, source_target_pairs={{0,4},{4,0},{8,12},{12,8},{1,5},{5,1},{9,13},{13,9},{2,6},{6,2},{1... | collective-permute-start | bytes 196616 | tf_op jit(solution)/shard_map/ppermute | solution.py:45
  8.3 1.5 %collective-permute-start = (f32[8,16,128]{2,1,0:T(8,128)S(1)}, f32[8,16,128]{2,1,0:T(8,128)S(1)}, u32[]{:S(2)}, u32[]{:S(2)}) collective-permute-start(f32[8,16,128]{2,1,0:T(8,128)S(1)} %bitcast.63), channel_id=1, source_target_pairs={{16,0},{0,16},{17,1},{1,17},{18,2},{2,18},{19,3},{3,19},{20,4},{4,... | collective-permute-start | bytes 196616 | tf_op jit(solution)/shard_map/ppermute | solution.py:42
  9.8 1.8 %dynamic-slice_bitcast_fusion = bf16[8,9,128,128]{3,2,1,0:T(8,128)(2,1)S(1)} fusion(bf16[1,1,16,9,128,128]{5,4,3,2,1,0:T(8,128)(2,1)} %param.2, s32[]{:T(128)S(6)} %select_n.36), kind=kLoop, calls=%fused_computation | loop fusion | bytes 4718596 | tf_op jit(solution)/shard_map/dynamic_slice | solution.py:51
  11.7 1.0 %bitcast_dynamic-update-slice_fusion.3 = bf16[8,9,128,128]{3,2,1,0:T(8,128)(2,1)S(1)} fusion(bf16[8,9,128,128]{3,2,1,0:T(8,128)(2,1)S(1)} %slice_dynamic-update-slice_fusion, bf16[1,1,16,9,128,128]{5,4,3,2,1,0:T(8,128)(2,1)} %param.2, s32[]{:T(128)S(6)} %select_n.37, s32[]{:T(128)S(6)} %select_n.40), kind=kLoop, calls=%fused_computation.5 | loop fusion | bytes 524296
  12.7 1.0 %bitcast_dynamic-update-slice_fusion.2 = bf16[8,9,128,128]{3,2,1,0:T(8,128)(2,1)S(1)} fusion(bf16[8,9,128,128]{3,2,1,0:T(8,128)(2,1)S(1)} %bitcast_dynamic-update-slice_fusion.3, bf16[1,1,16,9,128,128]{5,4,3,2,1,0:T(8,128)(2,1)} %param.2, s32[]{:T(128)S(6)} %select_n.37, s32[]{:T(128)S(6)} %select_n.42), kind=kLoop, calls=%fused_computation.4 | loop fusion | bytes 524296
  13.7 1.0 %bitcast_dynamic-update-slice_fusion.1 = bf16[8,9,128,128]{3,2,1,0:T(8,128)(2,1)S(1)} fusion(bf16[8,9,128,128]{3,2,1,0:T(8,128)(2,1)S(1)} %bitcast_dynamic-update-slice_fusion.2, bf16[1,1,16,9,128,128]{5,4,3,2,1,0:T(8,128)(2,1)} %param.2, s32[]{:T(128)S(6)} %select_n.37, s32[]{:T(128)S(6)} %select_n.45), kind=kLoop, calls=%fused_computation.3 | loop fusion | bytes 524296
  14.7 1.0 %bitcast_dynamic-update-slice_fusion = bf16[8,9,128,128]{3,2,1,0:T(8,128)(2,1)S(1)} fusion(bf16[8,9,128,128]{3,2,1,0:T(8,128)(2,1)S(1)} %bitcast_dynamic-update-slice_fusion.1, bf16[1,1,16,9,128,128]{5,4,3,2,1,0:T(8,128)(2,1)} %param.2, s32[]{:T(128)S(6)} %select_n.37, s32[]{:T(128)S(6)} %select_n.47), kind=kLoop, calls=%fused_computation.2 | loop fusion | bytes 524296 | tf_op jit(solution)/shard_map/concatenate | solution.py:60
  15.7 1.4 %copy-done = bf16[8,9,128,128]{3,2,1,0:T(8,128)(2,1)} copy-done((bf16[8,9,128,128]{3,2,1,0:T(8,128)(2,1)}, bf16[8,9,128,128]{3,2,1,0:T(8,128)(2,1)S(1)}, u32[]{:S(2)}) %copy-start) | copy-done | bytes 2359320
  17.1 3.0 %copy.27 = bf16[8,9,128,128]{3,2,1,0:T(8,128)(2,1)S(1)} copy(bf16[8,9,128,128]{2,3,1,0:T(8,128)(2,1)} %bitcast.78) | data formatting | bytes 4718592 | tf_op jit(solution)/shard_map/transpose | solution.py:61
  20.2 0.6 shard_map.41
  20.8 1.0 %collective-permute-start.9 = (f32[8,16,128]{2,1,0:T(8,128)S(1)}, f32[8,16,128]{2,1,0:T(8,128)S(1)}, u32[]{:S(2)}, u32[]{:S(2)}) collective-permute-start(f32[8,16,128]{2,1,0:T(8,128)S(1)} %get-tuple-element.19.refs_0_), channel_id=1, source_target_pairs={{0,3},{1,2},{2,1},{3,0},{4,7},{5,6},{6,5},{7,4},{8,11},{9,10},{10,... | collective-permute-start | bytes 196616 | tf_op jit(solution)/shard_map/ppermute | solution.py:45
  21.8 1.2 %collective-permute-start.8 = (f32[8,16,128]{2,1,0:T(8,128)S(1)}, f32[8,16,128]{2,1,0:T(8,128)S(1)}, u32[]{:S(2)}, u32[]{:S(2)}) collective-permute-start(f32[8,16,128]{2,1,0:T(8,128)S(1)} %get-tuple-element.19.refs_0_), channel_id=1, source_target_pairs={{0,1},{1,0},{2,3},{3,2},{4,5},{5,4},{6,7},{7,6},{8,9},{9,8},{10,11... | collective-permute-start | bytes 196616 | tf_op jit(solution)/shard_map/ppermute | solution.py:45
  22.9 0.6 collective-permute-start.6
  24.1 12.1 %all_to_all.44 = f32[32,1,128]{2,1,0:T(1,128)S(1)} all-to-all(f32[32,1,128]{2,1,0:T(1,128)S(1)} %bitcast.76), channel_id=1, replica_groups=mesh['grp'=2,'ta'=4,'gz'=4] {'grp','ta','gz'}, dimensions={0} | all-to-all | bytes 32768 | tf_op jit(solution)/shard_map/all_to_all | solution.py:229
  36.3 0.8 shard_map.42
  37.0 0.6 collective-permute-start.14
  37.6 0.5 collective-permute-start.13
  38.1 0.7 collective-permute-start.11
  38.8 0.6 collective-permute-start.10
  39.4 12.4 %all_to_all.45 = f32[32,1,128]{2,1,0:T(1,128)S(1)} all-to-all(f32[32,1,128]{2,1,0:T(1,128)S(1)} %bitcast.74), channel_id=1, replica_groups=mesh['grp'=2,'ta'=4,'gz'=4] {'grp','ta','gz'}, dimensions={0} | all-to-all | bytes 32768 | tf_op jit(solution)/shard_map/all_to_all | solution.py:229
  51.9 0.8 %shard_map.43 = (f32[8,16,128]{2,1,0:T(8,128)S(1)}, f32[32,128]{1,0:T(8,128)S(1)}, f32[6,8,16,128]{3,2,1,0:T(8,128)S(1)}, f32[6,8,16,128]{3,2,1,0:T(8,128)S(1)}) custom-call(bf16[8,1152,128]{2,1,0:T(8,128)(2,1)S(1)} %bitcast.57, f32[32,128]{1,0:T(8,128)S(1)} %bitcast.69, f32[8,16,128]{2,1,0:T(8,128)S(1)} %get-tuple-element.21.refs_0_, ...), custom_call_target="tpu_custom_call" | custom-call | flops 37748736 | bytes 4423680 | tf_op jit(solution)/shard_map/pallas_call | solution.py:217
  52.7 0.6 collective-permute-start.19
  53.3 0.5 collective-permute-start.18
  53.8 0.7 collective-permute-start.16
  54.5 0.6 collective-permute-start.15
  55.1 12.4 %all_to_all.46 = f32[32,1,128]{2,1,0:T(1,128)S(1)} all-to-all(f32[32,1,128]{2,1,0:T(1,128)S(1)} %bitcast.75), channel_id=1, replica_groups=mesh['grp'=2,'ta'=4,'gz'=4] {'grp','ta','gz'}, dimensions={0} | all-to-all | bytes 32768 | tf_op jit(solution)/shard_map/all_to_all | solution.py:229
  67.5 0.7 shard_map.44
  68.2 8.9 %all_to_all.47 = f32[32,1,128]{2,1,0:T(1,128)S(1)} all-to-all(f32[32,1,128]{2,1,0:T(1,128)S(1)} %bitcast.77), channel_id=1, replica_groups=mesh['grp'=2,'ta'=4,'gz'=4] {'grp','ta','gz'}, dimensions={0} | all-to-all | bytes 32768 | tf_op jit(solution)/shard_map/all_to_all | solution.py:229
  77.1 0.9 %shard_map.45 = (f32[16,8,128]{2,1,0:T(8,128)}, f32[16,8,128]{2,1,0:T(8,128)}) custom-call(f32[32,128]{1,0:T(8,128)S(1)} %bitcast.68, f32[32,128]{1,0:T(8,128)S(1)} %bitcast.70, f32[32,128]{1,0:T(8,128)S(1)} %bitcast.72, f32[32,128]{1,0:T(8,128)S(1)} %bitcast.73, f32[8,16,128]{2,1,0:T(8,128)S(1)} %get-tuple-element.29.refs_4_, f32[8,16,128]{2,1,0:T(8,128)S(1)} %bitcast.66, ...), custom_call_target="tpu_custom_call" | custom-call | flops 377487 | bytes 2686976 | tf_op jit(solution)/shard_map/pallas_call | solution.py:217
  (27 shorter events, 0.7 us)
Async XLA Ops:
  1.5 18.7 %collective-permute-start.4 = (f32[8,16,128]{2,1,0:T(8,128)S(1)}, f32[8,16,128]{2,1,0:T(8,128)S(1)}, u32[]{:S(2)}, u32[]{:S(2)}) collective-permute-start(f32[8,16,128]{2,1,0:T(8,128)S(1)} %bitcast.59), channel_id=1, source_target_pairs={{0,3},{1,2},{2,1},{3,0},{4,7},{5,6},{6,5},{7,4},{8,11},{9,10},{10,... | collective-permute-start | bytes 196616 | tf_op jit(solution)/shard_map/ppermute | solution.py:45
  6.6 13.6 %collective-permute-start.3 = (f32[8,16,128]{2,1,0:T(8,128)S(1)}, f32[8,16,128]{2,1,0:T(8,128)S(1)}, u32[]{:S(2)}, u32[]{:S(2)}) collective-permute-start(f32[8,16,128]{2,1,0:T(8,128)S(1)} %bitcast.60), channel_id=1, source_target_pairs={{0,1},{1,0},{2,3},{3,2},{4,5},{5,4},{6,7},{7,6},{8,9},{9,8},{10,11... | collective-permute-start | bytes 196616 | tf_op jit(solution)/shard_map/ppermute | solution.py:45
  6.6 13.6 %collective-permute-start.2 = (f32[8,16,128]{2,1,0:T(8,128)S(1)}, f32[8,16,128]{2,1,0:T(8,128)S(1)}, u32[]{:S(2)}, u32[]{:S(2)}) collective-permute-start(f32[8,16,128]{2,1,0:T(8,128)S(1)} %bitcast.61), channel_id=1, source_target_pairs={{0,12},{4,8},{8,4},{12,0},{1,13},{5,9},{9,5},{13,1},{2,14},{6,10},... | collective-permute-start | bytes 196616 | tf_op jit(solution)/shard_map/ppermute | solution.py:45
  7.3 12.9 %collective-permute-start.1 = (f32[8,16,128]{2,1,0:T(8,128)S(1)}, f32[8,16,128]{2,1,0:T(8,128)S(1)}, u32[]{:S(2)}, u32[]{:S(2)}) collective-permute-start(f32[8,16,128]{2,1,0:T(8,128)S(1)} %bitcast.62), channel_id=1, source_target_pairs={{0,4},{4,0},{8,12},{12,8},{1,5},{5,1},{9,13},{13,9},{2,6},{6,2},{1... | collective-permute-start | bytes 196616 | tf_op jit(solution)/shard_map/ppermute | solution.py:45
  8.3 12.0 %collective-permute-start = (f32[8,16,128]{2,1,0:T(8,128)S(1)}, f32[8,16,128]{2,1,0:T(8,128)S(1)}, u32[]{:S(2)}, u32[]{:S(2)}) collective-permute-start(f32[8,16,128]{2,1,0:T(8,128)S(1)} %bitcast.63), channel_id=1, source_target_pairs={{16,0},{0,16},{17,1},{1,17},{18,2},{2,18},{19,3},{3,19},{20,4},{4,... | collective-permute-start | bytes 196616 | tf_op jit(solution)/shard_map/ppermute | solution.py:42
  15.7 1.4 %copy-start = (bf16[8,9,128,128]{3,2,1,0:T(8,128)(2,1)}, bf16[8,9,128,128]{3,2,1,0:T(8,128)(2,1)S(1)}, u32[]{:S(2)}) copy-start(bf16[8,9,128,128]{3,2,1,0:T(8,128)(2,1)S(1)} %bitcast_dynamic-update-slice_fusion) | copy-start | bytes 7077892
  20.8 15.4 %collective-permute-start.9 = (f32[8,16,128]{2,1,0:T(8,128)S(1)}, f32[8,16,128]{2,1,0:T(8,128)S(1)}, u32[]{:S(2)}, u32[]{:S(2)}) collective-permute-start(f32[8,16,128]{2,1,0:T(8,128)S(1)} %get-tuple-element.19.refs_0_), channel_id=1, source_target_pairs={{0,3},{1,2},{2,1},{3,0},{4,7},{5,6},{6,5},{7,4},{8,11},{9,10},{10,... | collective-permute-start | bytes 196616 | tf_op jit(solution)/shard_map/ppermute | solution.py:45
  21.8 14.5 %collective-permute-start.8 = (f32[8,16,128]{2,1,0:T(8,128)S(1)}, f32[8,16,128]{2,1,0:T(8,128)S(1)}, u32[]{:S(2)}, u32[]{:S(2)}) collective-permute-start(f32[8,16,128]{2,1,0:T(8,128)S(1)} %get-tuple-element.19.refs_0_), channel_id=1, source_target_pairs={{0,1},{1,0},{2,3},{3,2},{4,5},{5,4},{6,7},{7,6},{8,9},{9,8},{10,11... | collective-permute-start | bytes 196616 | tf_op jit(solution)/shard_map/ppermute | solution.py:45
  22.9 13.3 %collective-permute-start.7 = (f32[8,16,128]{2,1,0:T(8,128)S(1)}, f32[8,16,128]{2,1,0:T(8,128)S(1)}, u32[]{:S(2)}, u32[]{:S(2)}) collective-permute-start(f32[8,16,128]{2,1,0:T(8,128)S(1)} %get-tuple-element.19.refs_0_), channel_id=1, source_target_pairs={{0,12},{4,8},{8,4},{12,0},{1,13},{5,9},{9,5},{13,1},{2,14},{6,10},... | collective-permute-start | bytes 196616 | tf_op jit(solution)/shard_map/ppermute | solution.py:45
  22.9 13.3 %collective-permute-start.6 = (f32[8,16,128]{2,1,0:T(8,128)S(1)}, f32[8,16,128]{2,1,0:T(8,128)S(1)}, u32[]{:S(2)}, u32[]{:S(2)}) collective-permute-start(f32[8,16,128]{2,1,0:T(8,128)S(1)} %get-tuple-element.19.refs_0_), channel_id=1, source_target_pairs={{0,4},{4,0},{8,12},{12,8},{1,5},{5,1},{9,13},{13,9},{2,6},{6,2},{1... | collective-permute-start | bytes 196616 | tf_op jit(solution)/shard_map/ppermute | solution.py:45
  23.6 12.7 %collective-permute-start.5 = (f32[8,16,128]{2,1,0:T(8,128)S(1)}, f32[8,16,128]{2,1,0:T(8,128)S(1)}, u32[]{:S(2)}, u32[]{:S(2)}) collective-permute-start(f32[8,16,128]{2,1,0:T(8,128)S(1)} %get-tuple-element.19.refs_0_), channel_id=1, source_target_pairs={{16,0},{0,16},{17,1},{1,17},{18,2},{2,18},{19,3},{3,19},{20,4},{4,... | collective-permute-start | bytes 196616 | tf_op jit(solution)/shard_map/ppermute | solution.py:42
  37.0 14.8 %collective-permute-start.14 = (f32[8,16,128]{2,1,0:T(8,128)S(1)}, f32[8,16,128]{2,1,0:T(8,128)S(1)}, u32[]{:S(2)}, u32[]{:S(2)}) collective-permute-start(f32[8,16,128]{2,1,0:T(8,128)S(1)} %get-tuple-element.21.refs_0_), channel_id=1, source_target_pairs={{0,3},{1,2},{2,1},{3,0},{4,7},{5,6},{6,5},{7,4},{8,11},{9,10},{10,... | collective-permute-start | bytes 196616 | tf_op jit(solution)/shard_map/ppermute | solution.py:45
  37.6 14.2 %collective-permute-start.13 = (f32[8,16,128]{2,1,0:T(8,128)S(1)}, f32[8,16,128]{2,1,0:T(8,128)S(1)}, u32[]{:S(2)}, u32[]{:S(2)}) collective-permute-start(f32[8,16,128]{2,1,0:T(8,128)S(1)} %get-tuple-element.21.refs_0_), channel_id=1, source_target_pairs={{0,1},{1,0},{2,3},{3,2},{4,5},{5,4},{6,7},{7,6},{8,9},{9,8},{10,11... | collective-permute-start | bytes 196616 | tf_op jit(solution)/shard_map/ppermute | solution.py:45
  38.1 13.7 %collective-permute-start.12 = (f32[8,16,128]{2,1,0:T(8,128)S(1)}, f32[8,16,128]{2,1,0:T(8,128)S(1)}, u32[]{:S(2)}, u32[]{:S(2)}) collective-permute-start(f32[8,16,128]{2,1,0:T(8,128)S(1)} %get-tuple-element.21.refs_0_), channel_id=1, source_target_pairs={{0,12},{4,8},{8,4},{12,0},{1,13},{5,9},{9,5},{13,1},{2,14},{6,10},... | collective-permute-start | bytes 196616 | tf_op jit(solution)/shard_map/ppermute | solution.py:45
  38.1 13.7 %collective-permute-start.11 = (f32[8,16,128]{2,1,0:T(8,128)S(1)}, f32[8,16,128]{2,1,0:T(8,128)S(1)}, u32[]{:S(2)}, u32[]{:S(2)}) collective-permute-start(f32[8,16,128]{2,1,0:T(8,128)S(1)} %get-tuple-element.21.refs_0_), channel_id=1, source_target_pairs={{0,4},{4,0},{8,12},{12,8},{1,5},{5,1},{9,13},{13,9},{2,6},{6,2},{1... | collective-permute-start | bytes 196616 | tf_op jit(solution)/shard_map/ppermute | solution.py:45
  38.8 13.0 %collective-permute-start.10 = (f32[8,16,128]{2,1,0:T(8,128)S(1)}, f32[8,16,128]{2,1,0:T(8,128)S(1)}, u32[]{:S(2)}, u32[]{:S(2)}) collective-permute-start(f32[8,16,128]{2,1,0:T(8,128)S(1)} %get-tuple-element.21.refs_0_), channel_id=1, source_target_pairs={{16,0},{0,16},{17,1},{1,17},{18,2},{2,18},{19,3},{3,19},{20,4},{4,... | collective-permute-start | bytes 196616 | tf_op jit(solution)/shard_map/ppermute | solution.py:42
  52.7 14.8 %collective-permute-start.19 = (f32[8,16,128]{2,1,0:T(8,128)S(1)}, f32[8,16,128]{2,1,0:T(8,128)S(1)}, u32[]{:S(2)}, u32[]{:S(2)}) collective-permute-start(f32[8,16,128]{2,1,0:T(8,128)S(1)} %get-tuple-element.25.refs_0_), channel_id=1, source_target_pairs={{0,3},{1,2},{2,1},{3,0},{4,7},{5,6},{6,5},{7,4},{8,11},{9,10},{10,... | collective-permute-start | bytes 196616 | tf_op jit(solution)/shard_map/ppermute | solution.py:45
  53.3 14.2 %collective-permute-start.18 = (f32[8,16,128]{2,1,0:T(8,128)S(1)}, f32[8,16,128]{2,1,0:T(8,128)S(1)}, u32[]{:S(2)}, u32[]{:S(2)}) collective-permute-start(f32[8,16,128]{2,1,0:T(8,128)S(1)} %get-tuple-element.25.refs_0_), channel_id=1, source_target_pairs={{0,1},{1,0},{2,3},{3,2},{4,5},{5,4},{6,7},{7,6},{8,9},{9,8},{10,11... | collective-permute-start | bytes 196616 | tf_op jit(solution)/shard_map/ppermute | solution.py:45
  53.8 13.7 %collective-permute-start.17 = (f32[8,16,128]{2,1,0:T(8,128)S(1)}, f32[8,16,128]{2,1,0:T(8,128)S(1)}, u32[]{:S(2)}, u32[]{:S(2)}) collective-permute-start(f32[8,16,128]{2,1,0:T(8,128)S(1)} %get-tuple-element.25.refs_0_), channel_id=1, source_target_pairs={{0,12},{4,8},{8,4},{12,0},{1,13},{5,9},{9,5},{13,1},{2,14},{6,10},... | collective-permute-start | bytes 196616 | tf_op jit(solution)/shard_map/ppermute | solution.py:45
  53.8 13.7 %collective-permute-start.16 = (f32[8,16,128]{2,1,0:T(8,128)S(1)}, f32[8,16,128]{2,1,0:T(8,128)S(1)}, u32[]{:S(2)}, u32[]{:S(2)}) collective-permute-start(f32[8,16,128]{2,1,0:T(8,128)S(1)} %get-tuple-element.25.refs_0_), channel_id=1, source_target_pairs={{0,4},{4,0},{8,12},{12,8},{1,5},{5,1},{9,13},{13,9},{2,6},{6,2},{1... | collective-permute-start | bytes 196616 | tf_op jit(solution)/shard_map/ppermute | solution.py:45
  54.5 13.0 %collective-permute-start.15 = (f32[8,16,128]{2,1,0:T(8,128)S(1)}, f32[8,16,128]{2,1,0:T(8,128)S(1)}, u32[]{:S(2)}, u32[]{:S(2)}) collective-permute-start(f32[8,16,128]{2,1,0:T(8,128)S(1)} %get-tuple-element.25.refs_0_), channel_id=1, source_target_pairs={{16,0},{0,16},{17,1},{1,17},{18,2},{2,18},{19,3},{3,19},{20,4},{4,... | collective-permute-start | bytes 196616 | tf_op jit(solution)/shard_map/ppermute | solution.py:42

commit v2 on v1

v2 whole, which is shorter than its diff:
```python
import functools

import jax
import jax.numpy as jnp
import numpy as np
from jax import lax
from jax.experimental import pallas as pl
from jax.experimental.pallas import tpu as pltpu
from jax.sharding import PartitionSpec as P


LX = 4
LY = 4
ITERS = 4
AXES = ("grp", "ta", "gz")
LANES = 128
GRANT = 16 * 1024 * 1024
CHIP_ROOM = 9400 * 1024


def site_table():
    site_ids = np.arange(LX * LY)
    column = site_ids % LX
    row_of = site_ids // LX
    forward_x = row_of * LX + (column + 1) % LX
    backward_x = row_of * LX + (column - 1) % LX
    forward_y = (row_of + 1) % LY * LX + column
    backward_y = (row_of - 1) % LY * LX + column
    return np.stack([forward_x, backward_x, forward_y, backward_y], axis=1).astype(np.int32)


def pairings(count):
    if count % 2 == 0:
        first = [(i, i ^ 1) for i in range(count)]
        second = [(i, (i + 1) % count if i % 2 else (i - 1) % count) for i in range(count)]
        return first, second, True
    up = [((i + 1) % count, i) for i in range(count)]
    return up, [(target, source) for source, target in up], False


def exchange(block):
    count = lax.axis_size("grp")
    blocks = []
    for shift in range(1, count):
        pairs = [((i + shift) % count, i) for i in range(count)]
        blocks.append(lax.ppermute(block, "grp", pairs))
    for axis in ("ta", "gz"):
        first, second, _ = pairings(lax.axis_size(axis))
        for pairs in (first, second):
            blocks.append(lax.ppermute(block, axis, pairs))
    return blocks


def link_places():
    order = [0, 1, 2, 3, 4]
    for axis, base in (("ta", 7), ("gz", 5)):
        odd = lax.axis_index(axis) % 2 if pairings(lax.axis_size(axis))[2] else 0
        order += [base + odd, base + 1 - odd]
    return order


def arrange_kernel(held, links_ref, *refs):
    *outs, raw, turned, arrived, left = refs
    count = raw.shape[0]
    offset = lax.axis_index("grp") * count
    order = link_places()
    width = raw.shape[2]
    incoming = [
        pltpu.make_async_copy(links_ref.at[offset + site], raw.at[site], arrived.at[site])
        for site in range(count)
    ]
    for copy in incoming:
        copy.start()
    outgoing = []
    for site in reversed(range(count)):
        incoming[site].wait()
        target = outs[0].at[site] if site < held else turned.at[site - held]
        for place, hop in enumerate(order):
            target[place * width : (place + 1) * width, :] = raw[site, hop].T
        if site >= held:
            place = site - held
            copy = pltpu.make_async_copy(target, outs[-1].at[place], left.at[place])
            copy.start()
            outgoing.append(copy)
    for copy in outgoing:
        copy.wait()


def arranged_links(links, count, held):
    _, hops, width, depth = links.shape
    site = (hops * depth, width)
    rest = count - held
    vmem, hbm = pl.BlockSpec(memory_space=pltpu.VMEM), pl.BlockSpec(memory_space=pltpu.HBM)
    outs, specs = [], []
    if held:
        outs.append(jax.ShapeDtypeStruct((held,) + site, links.dtype))
        specs.append(vmem)
    if rest:
        outs.append(pltpu.HBM((rest,) + site, links.dtype))
        specs.append(hbm)
    size = 2 * count * int(np.prod(site)) * links.dtype.itemsize
    return pl.pallas_call(
        functools.partial(arrange_kernel, held),
        out_shape=tuple(outs),
        in_specs=[hbm],
        out_specs=tuple(specs),
        scratch_shapes=[
            pltpu.VMEM((count,) + links.shape[1:], links.dtype),
            pltpu.VMEM((max(rest, 1),) + site, links.dtype),
            pltpu.SemaphoreType.DMA((count,)),
            pltpu.SemaphoreType.DMA((max(rest, 1),)),
        ],
        compiler_params=pltpu.CompilerParams(vmem_limit_bytes=GRANT),
        cost_estimate=pl.CostEstimate(flops=0, bytes_accessed=size, transcendentals=0),
    )(pltpu.with_memory_space_constraint(links, pltpu.HBM))


class Field:
    def __init__(self, ref, given=None):
        self.ref = ref
        self.given = given

    def place(self, site):
        if self.given is None:
            return site
        return pl.ds(site, self.ref.shape[0] // self.given, stride=self.given)

    def __getitem__(self, site):
        return self.ref[self.place(site)]

    def __setitem__(self, site, value):
        self.ref[self.place(site)] = value


def columns(gathered, count, rhs):
    total = jnp.sum(gathered, axis=0, keepdims=True)
    spread = jnp.broadcast_to(total, (rhs, total.shape[1]))
    lane = lax.broadcasted_iota(jnp.int32, spread.shape, 1)
    row = lax.broadcasted_iota(jnp.int32, spread.shape, 0)
    return [
        jnp.sum(jnp.where(lane == row + index * rhs, spread, 0.0), axis=1, keepdims=True)
        for index in range(count)
    ]


def weights(gathered, previous, rhs):
    values = columns(gathered, previous + 2, rhs)
    coefficients = values[:previous]
    squared, projected = values[previous], values[previous + 1]
    for value in coefficients:
        squared = squared - value * value
    inverse = 1.0 / jnp.sqrt(squared)
    return coefficients, inverse, projected * inverse


class Links:
    def __init__(self, rows, refs, landing, arrived):
        self.held = rows["held"]
        self.chip = refs[0] if self.held else None
        self.landing = landing
        self.copies = []
        for place in range(rows["sites"] - self.held):
            copy = pltpu.make_async_copy(refs[-1].at[place], landing.at[place], arrived.at[place])
            copy.start()
            self.copies.append(copy)

    def __getitem__(self, site):
        if site < self.held:
            return self.chip[site]
        self.copies[site - self.held].wait()
        return self.landing[site - self.held]


def products(rows, links, table_ref, plane_ref, blocks):
    plane = [value for block in blocks[: rows["plane"]] for value in block]
    neighbours = rows["neighbours"]
    if neighbours is None:
        for index, value in enumerate(plane):
            plane_ref[index] = value
    result = []
    for site in range(rows["sites"]):
        parts = [blocks[0][site]]
        if neighbours is None:
            parts += [plane_ref[table_ref[site, hop]] for hop in range(4)]
        else:
            parts += [plane[index] for index in neighbours[site]]
        parts += [block[site] for block in blocks[rows["plane"] :]]
        result.append(
            jnp.dot(
                jnp.concatenate(parts, axis=1), links[site], preferred_element_type=jnp.float32
            )
        )
    return result


def inner_rows(pairs, out_ref):
    stacked = []
    for left, right in pairs:
        total = left[0] * right[0]
        for a, b in zip(left[1:], right[1:]):
            total = total + a * b
        stacked.append(total)
    height = sum(value.shape[0] for value in stacked)
    if out_ref.shape[1] > height:
        stacked.append(jnp.zeros((out_ref.shape[1] - height, stacked[0].shape[1]), jnp.float32))
    table = jnp.concatenate(stacked, axis=0)
    ones = jnp.ones((out_ref.shape[0], table.shape[1]), jnp.float32)
    out_ref[...] = lax.dot_general(
        ones,
        table,
        (((1,), (1,)), ((), ())),
        precision=lax.Precision.HIGHEST,
        preferred_element_type=jnp.float32,
    )


def first_kernel(rows, *refs):
    refs = list(refs)
    *refs, plane_ref, landing, arrived = refs
    table_ref, refs = (None, refs) if rows["neighbours"] else (refs[0], refs[1:])
    links = Links(rows, refs[: rows["parts"]], landing, arrived)
    *residual_refs, mapped_ref, dots_ref = refs[rows["parts"] :]
    sites = range(rows["sites"])
    residual_refs = [Field(ref, rows["sites"]) for ref in residual_refs]
    blocks = [[ref[site].astype(jnp.bfloat16) for site in sites] for ref in residual_refs]
    mapped = products(rows, links, table_ref, plane_ref, blocks)
    own = [residual_refs[0][site] for site in sites]
    for site in sites:
        mapped_ref[site] = mapped[site]
    inner_rows([(mapped, mapped), (mapped, own)], dots_ref)


def next_kernel(rows, previous, *refs):
    refs = list(refs)
    *refs, plane_ref, landing, arrived = refs
    table_ref, refs = (None, refs) if rows["neighbours"] else (refs[0], refs[1:])
    links = Links(rows, refs[: rows["parts"]], landing, arrived)
    gathered_ref, *refs = refs[rows["parts"] :]
    count = rows["blocks"]
    sites = range(rows["sites"])

    def field(stacked):
        own = refs.pop(0)
        if stacked:
            halo = refs.pop(0)
            return [own] + [halo.at[index] for index in range(count - 1)]
        return [own] + [refs.pop(0) for _ in range(count - 1)]

    mapped_in = field(False)
    residual_in = field(previous > 0)
    if previous == 0:
        residual_in = [Field(ref, rows["sites"]) for ref in residual_in]
    basis = [field(True) for _ in range(previous)]
    mapped_ref, dots_ref = refs.pop(0), refs.pop(0)
    keep_halo = previous < ITERS - 2
    outs = [field(True) if keep_halo else [refs.pop(0)] for _ in range(2)]
    rhs = mapped_in[0].shape[1]
    coefficients, inverse, alpha = weights(gathered_ref[...], previous, rhs)
    blocks = []
    own = []
    for index in range(count):
        block = []
        for site in sites:
            q = mapped_in[index][site]
            for weight, older in zip(coefficients, basis):
                q = q - weight * older[index][site]
            q = q * inverse
            residual = residual_in[index][site] - alpha * q
            if keep_halo or index == 0:
                outs[0][index][site] = residual
                outs[1][index][site] = q
            block.append(residual.astype(jnp.bfloat16))
            if index == 0:
                own.append(residual)
        blocks.append(block)
    mapped = products(rows, links, table_ref, plane_ref, blocks)
    for site in sites:
        mapped_ref[site] = mapped[site]
    pairs = [
        ([older[site] for site in sites], mapped)
        for older in [field_refs[0] for field_refs in basis] + [outs[1][0]]
    ]
    inner_rows(pairs + [(mapped, mapped), (mapped, own)], dots_ref)


def last_kernel(rows, last, *refs):
    gathered, refs = refs[: last + 1], refs[last + 1 :]
    mapped_ref, refs = refs[0], refs[1:]
    residuals, basis, (solution_ref, residual_ref) = (
        refs[: last + 1],
        refs[last + 1 : 2 * last + 1],
        refs[2 * last + 1 :],
    )
    residuals = [Field(residuals[0], rows["sites"])] + list(residuals[1:])
    solution_ref, residual_ref = (Field(ref, rows["sites"]) for ref in (solution_ref, residual_ref))
    rhs = mapped_ref.shape[1]
    steps = [weights(ref[...], index, rhs) for index, ref in enumerate(gathered)]
    coefficients, inverse, alpha = steps[last]
    for site in range(rows["sites"]):
        q = mapped_ref[site]
        for weight, older in zip(coefficients, basis):
            q = q - weight * older[site]
        q = q * inverse
        residual_ref[site] = residuals[last][site] - alpha * q
        found = []
        solution = None
        for index in range(last + 1):
            p = residuals[index][site].astype(jnp.bfloat16).astype(jnp.float32)
            for weight, older in zip(steps[index][0], found):
                p = p - weight * older
            p = p * steps[index][1]
            found.append(p)
            term = steps[index][2] * p
            solution = term if solution is None else solution + term
        solution_ref[site] = solution


def call(body, outs, operands, flops, links=(), table=None, scratch=()):
    vmem = pl.BlockSpec(memory_space=pltpu.VMEM)
    specs = [vmem] * len(operands)
    lead, lead_specs = [], []
    if table is not None:
        lead.append(table)
        lead_specs.append(pl.BlockSpec(memory_space=pltpu.SMEM))
    for value, on_chip in links:
        lead.append(value if on_chip else pltpu.with_memory_space_constraint(value, pltpu.HBM))
        lead_specs.append(vmem if on_chip else pl.BlockSpec(memory_space=pltpu.HBM))
    size = sum(int(np.prod(v.shape)) * v.dtype.itemsize for v in list(outs) + list(operands))
    return pl.pallas_call(
        body,
        out_shape=tuple(outs),
        in_specs=lead_specs + specs,
        out_specs=tuple([vmem] * len(outs)),
        scratch_shapes=list(scratch),
        compiler_params=pltpu.CompilerParams(vmem_limit_bytes=GRANT),
        cost_estimate=pl.CostEstimate(flops=flops, bytes_accessed=size, transcendentals=0),
    )(*lead, *operands)


def gather_all(dots):
    return lax.all_to_all(dots, AXES, 0, 0, tiled=True)


def local(coarse_links, right_sides):
    f32 = jnp.float32
    rhs, _, _, site_count, width = right_sides.shape
    hops = coarse_links.shape[3]
    group = lax.axis_size("grp")
    devices = group * lax.axis_size("ta") * lax.axis_size("gz")
    blocks = group + 4
    own = right_sides.reshape(rhs * site_count, width)
    table = site_table()
    field_bytes = site_count * rhs * width * 4
    site_bytes = hops * width * width * coarse_links.dtype.itemsize
    room = CHIP_ROOM - (ITERS * blocks + ITERS) * field_bytes
    held = max(0, min(site_count, room // site_bytes))
    rows = {
        "plane": group,
        "sites": site_count,
        "blocks": blocks,
        "neighbours": None,
        "held": held,
        "parts": (held > 0) + (held < site_count),
    }
    dynamic = None
    if site_count % LX == 0:
        rows["neighbours"] = table[:site_count].tolist()
    else:
        offset = lax.axis_index("grp") * site_count
        places = lax.dynamic_slice_in_dim(jnp.asarray(table), offset, site_count, 0)
        dynamic = (places - offset + table.shape[0]) % table.shape[0]
    halo = exchange(own)
    parts = arranged_links(coarse_links[0, 0], site_count, held)
    links = [(value, held > 0 and index == 0) for index, value in enumerate(parts)]
    flops = 2 * site_count * hops * width * width * rhs
    rest = max(site_count - held, 1)
    scratch = [
        pltpu.VMEM((group * site_count, rhs, width), jnp.bfloat16),
        pltpu.VMEM((rest, hops * width, width), coarse_links.dtype),
        pltpu.SemaphoreType.DMA((rest,)),
    ]
    one = jax.ShapeDtypeStruct((site_count, rhs, width), f32)
    several = jax.ShapeDtypeStruct((blocks - 1, site_count, rhs, width), f32)

    def dots_shape(count):
        return jax.ShapeDtypeStruct((devices, -(-count * rhs // LANES) * LANES), f32)

    mapped, dots = call(
        functools.partial(first_kernel, rows),
        [one, dots_shape(2)],
        [own] + halo,
        flops,
        links,
        dynamic,
        scratch,
    )
    gathered = []
    residuals = [[own] + halo]
    basis = []
    for previous in range(ITERS - 1):
        gathered.append(gather_all(dots))
        halo = exchange(mapped)
        kept = [one, several] if previous < ITERS - 2 else [one]
        mapped, dots, *rest = call(
            functools.partial(next_kernel, rows, previous),
            [one, dots_shape(previous + 3)] + kept + kept,
            [gathered[-1], mapped] + halo + residuals[-1] + [ref for pair in basis for ref in pair],
            flops,
            links,
            dynamic,
            scratch,
        )
        residuals.append(rest[: len(kept)])
        basis.append(rest[len(kept) :])
    gathered.append(gather_all(dots))
    out = jax.ShapeDtypeStruct(own.shape, f32)
    found, left = call(
        functools.partial(last_kernel, rows, ITERS - 1),
        [out, out],
        gathered + [mapped] + [pair[0] for pair in residuals] + [pair[0] for pair in basis],
        flops // 100,
    )
    return (found.reshape(right_sides.shape), left.reshape(right_sides.shape))


def solution(mesh):
    placed = (P("ta", "gz", None, None, None, None), P(None, "ta", "gz", "grp", None))
    return jax.shard_map(
        local,
        mesh=mesh,
        in_specs=placed,
        out_specs=(P(None, "ta", "gz", "grp", None), P(None, "ta", "gz", "grp", None)),
        check_vma=False,
    )
```

time: 78.5 us -> 70.2 us (0.89)
  local copies, waits for them, and re-layouts: 11.2 us -> 0.01 us
  Pallas kernels: 3.78 us -> 6.67 us
  starting transfers between devices: 16.4 us -> 17.4 us
  blocking collectives: 45.8 us -> 44.9 us
    unnamed x7 -> x2, local copies, waits for them, and re-layouts: 5.36 us -> 0.01 us
    transpose x1 -> x0, local copies, waits for them, and re-layouts: 3.05 us -> none  [arranged_links(): return jnp.swapaxes(ordered, 2, 3).reshape(site_count, -1, ordered.shape[2])]
    pallas_call x5 -> x6, Pallas kernels: 3.78 us -> 6.67 us  [the longest x5 3.9 us: call(): pl.pallas_call(body, out_shape=tuple(outs), in_specs=lead_specs + specs,...]
    dynamic_slice x1 -> x0, local copies, waits for them, and re-layouts: 1.82 us -> none  [arranged_links(): part = lax.dynamic_slice_in_dim(coarse_links[0, 0], offset, site_count, 0)]
    ppermute x20, starting transfers between devices: 16.4 us -> 17.4 us  [the longest x16 13.3 us: exchange(): blocks.append(lax.ppermute(block, axis, pairs))]
    concatenate x1 -> x0, local copies, waits for them, and re-layouts: 1 us -> none  [arranged_links(): ordered = jnp.concatenate(pieces, axis=1)]
    all_to_all x4, blocking collectives: 45.8 us -> 44.9 us  [gather_all(): return lax.all_to_all(dots, AXES, 0, 0, tiled=True)]
  transfers between devices with their start and end apart: 20 -> 20, of which waited for: 0 -> 1; matrix products, arithmetic and copies ran while one was open for 11% -> 0% of each run, Pallas kernels for 0% -> 4%
where the time goes in v2:
time: 70.2 us; the launch traced here: 70 us
  blocking collectives  44.9 us (64%)
  starting transfers between devices  17.4 us (25%)
  Pallas kernels  6.67 us (10%)
  between operations  0.78 us (1%)
    all_to_all x4, blocking collectives, gather_all(): return lax.all_to_all(dots, AXES, 0, 0, tiled=True)  44.9 us
    ppermute x16, starting transfers between devices, exchange(): blocks.append(lax.ppermute(block, axis, pairs))  13.3 us
    ppermute x4, starting transfers between devices, exchange(): blocks.append(lax.ppermute(block, 'grp', pairs))  4.16 us
    pallas_call x5, Pallas kernels, call(): pl.pallas_call(body, out_shape=tuple(outs), in_specs=lead_specs + specs,...  3.9 us
    pallas_call x1, Pallas kernels, arranged_links(): pl.pallas_call(functools.partial(arrange_kernel, held), out_shape=tuple(o...  2.77 us
  transfers between devices with their start and end apart: 20, of which 1 were waited for; matrix products, arithmetic and copies ran while one was open for 0% of the time, Pallas kernels for 4%

profile of v2, /device:TPU:0, one launch (start us, length us, event | category | flops | bytes accessed | tf_op | source)
XLA Modules:
  0.0 70.0 jit_solution(10048495573842994731)
XLA Ops:
  0.6 5.1 %collective-permute-start.4 = (f32[128,128]{1,0:T(8,128)}, f32[128,128]{1,0:T(8,128)S(1)}, u32[]{:S(2)}, u32[]{:S(2)}) collective-permute-start(f32[128,128]{1,0:T(8,128)} %bitcast.24), channel_id=1, source_target_pairs={{0,3},{1,2},{2,1},{3,0},{4,7},{5,6},{6,5},{7,4},{8,11},{9,10},{10,... | collective-permute-start | bytes 196616 | tf_op jit(solution)/shard_map/ppermute | solution.py:50
  5.8 0.0 collective-permute-start.3
  5.8 0.7 collective-permute-start.2
  6.5 1.0 %collective-permute-start.1 = (f32[128,128]{1,0:T(8,128)}, f32[128,128]{1,0:T(8,128)S(1)}, u32[]{:S(2)}, u32[]{:S(2)}) collective-permute-start(f32[128,128]{1,0:T(8,128)} %bitcast.27), channel_id=1, source_target_pairs={{0,4},{4,0},{8,12},{12,8},{1,5},{5,1},{9,13},{13,9},{2,6},{6,2},{1... | collective-permute-start | bytes 196616 | tf_op jit(solution)/shard_map/ppermute | solution.py:50
  7.4 1.5 %collective-permute-start = (f32[128,128]{1,0:T(8,128)}, f32[128,128]{1,0:T(8,128)S(1)}, u32[]{:S(2)}, u32[]{:S(2)}) collective-permute-start(f32[128,128]{1,0:T(8,128)} %bitcast.28), channel_id=1, source_target_pairs={{16,0},{0,16},{17,1},{1,17},{18,2},{2,18},{19,3},{3,19},{20,4},{4,... | collective-permute-start | bytes 196616 | tf_op jit(solution)/shard_map/ppermute | solution.py:46
  8.9 2.8 %shard_map.41.refs_0_ = bf16[8,1152,128]{2,1,0:T(8,128)(2,1)S(1)} custom-call(bf16[16,9,128,128]{3,2,1,0:T(8,128)(2,1)} %bitcast.43), custom_call_target="tpu_custom_call" | custom-call | bytes 4718592 | tf_op jit(solution)/shard_map/pallas_call | solution.py:102
  11.7 0.0 collective-permute-done.4.refs_6_.refs_13_
  11.7 0.0 collective-permute-done.3.refs_5_.refs_12_
  11.7 0.0 collective-permute-done.1.refs_3_.refs_10_
  11.7 0.2 collective-permute-done.refs_2_.refs_9_
  11.9 0.7 shard_map.42
  12.6 1.0 %collective-permute-start.9 = (f32[8,16,128]{2,1,0:T(8,128)S(1)}, f32[8,16,128]{2,1,0:T(8,128)S(1)}, u32[]{:S(2)}, u32[]{:S(2)}) collective-permute-start(f32[8,16,128]{2,1,0:T(8,128)S(1)} %get-tuple-element.23.refs_2_), channel_id=1, source_target_pairs={{0,3},{1,2},{2,1},{3,0},{4,7},{5,6},{6,5},{7,4},{8,11},{9,10},{10,... | collective-permute-start | bytes 196616 | tf_op jit(solution)/shard_map/ppermute | solution.py:50
  13.5 1.2 %collective-permute-start.8 = (f32[8,16,128]{2,1,0:T(8,128)S(1)}, f32[8,16,128]{2,1,0:T(8,128)S(1)}, u32[]{:S(2)}, u32[]{:S(2)}) collective-permute-start(f32[8,16,128]{2,1,0:T(8,128)S(1)} %get-tuple-element.23.refs_2_), channel_id=1, source_target_pairs={{0,1},{1,0},{2,3},{3,2},{4,5},{5,4},{6,7},{7,6},{8,9},{9,8},{10,11... | collective-permute-start | bytes 196616 | tf_op jit(solution)/shard_map/ppermute | solution.py:50
  14.7 0.6 collective-permute-start.6
  15.4 1.5 %collective-permute-start.5 = (f32[8,16,128]{2,1,0:T(8,128)S(1)}, f32[8,16,128]{2,1,0:T(8,128)S(1)}, u32[]{:S(2)}, u32[]{:S(2)}) collective-permute-start(f32[8,16,128]{2,1,0:T(8,128)S(1)} %get-tuple-element.23.refs_2_), channel_id=1, source_target_pairs={{16,0},{0,16},{17,1},{1,17},{18,2},{2,18},{19,3},{3,19},{20,4},{4,... | collective-permute-start | bytes 196616 | tf_op jit(solution)/shard_map/ppermute | solution.py:46
  16.8 11.2 %all_to_all.44 = f32[32,1,128]{2,1,0:T(1,128)S(1)} all-to-all(f32[32,1,128]{2,1,0:T(1,128)S(1)} %bitcast.41), channel_id=1, replica_groups=mesh['grp'=2,'ta'=4,'gz'=4] {'grp','ta','gz'}, dimensions={0} | all-to-all | bytes 32768 | tf_op jit(solution)/shard_map/all_to_all | solution.py:341
  28.0 0.0 collective-permute-done.6.refs_4_
  28.0 0.8 %shard_map.43 = (f32[8,16,128]{2,1,0:T(8,128)S(1)}, f32[32,128]{1,0:T(8,128)S(1)}, f32[8,16,128]{2,1,0:T(8,128)S(1)}, f32[5,8,16,128]{3,2,1,0:T(8,128)S(1)}, f32...) custom-call(bf16[8,1152,128]{2,1,0:T(8,128)(2,1)S(1)} %shard_map.41.refs_0_, f32[32,128]{1,0:T(8,128)S(1)} %bitcast.32, ...), custom_call_target="tpu_custom_call" | custom-call | flops 37748736 | bytes 1671168 | tf_op jit(solution)/shard_map/pallas_call | solution.py:329
  28.8 0.6 collective-permute-start.14
  29.5 0.5 collective-permute-start.13
  30.0 0.7 collective-permute-start.11
  30.7 0.6 collective-permute-start.10
  31.3 12.4 %all_to_all.45 = f32[32,1,128]{2,1,0:T(1,128)S(1)} all-to-all(f32[32,1,128]{2,1,0:T(1,128)S(1)} %bitcast.39), channel_id=1, replica_groups=mesh['grp'=2,'ta'=4,'gz'=4] {'grp','ta','gz'}, dimensions={0} | all-to-all | bytes 32768 | tf_op jit(solution)/shard_map/all_to_all | solution.py:341
  43.7 0.8 %shard_map.44 = (f32[8,16,128]{2,1,0:T(8,128)S(1)}, f32[32,128]{1,0:T(8,128)S(1)}, f32[8,16,128]{2,1,0:T(8,128)S(1)}, f32[5,8,16,128]{3,2,1,0:T(8,128)S(1)}, f32...) custom-call(bf16[8,1152,128]{2,1,0:T(8,128)(2,1)S(1)} %shard_map.41.refs_0_, f32[32,128]{1,0:T(8,128)S(1)} %bitcast.34, ...), custom_call_target="tpu_custom_call" | custom-call | flops 37748736 | bytes 2064384 | tf_op jit(solution)/shard_map/pallas_call | solution.py:329
  44.6 0.6 collective-permute-start.19
  45.2 0.5 collective-permute-start.18
  45.8 0.7 collective-permute-start.16
  46.4 0.6 collective-permute-start.15
  47.0 12.4 %all_to_all.46 = f32[32,1,128]{2,1,0:T(1,128)S(1)} all-to-all(f32[32,1,128]{2,1,0:T(1,128)S(1)} %bitcast.40), channel_id=1, replica_groups=mesh['grp'=2,'ta'=4,'gz'=4] {'grp','ta','gz'}, dimensions={0} | all-to-all | bytes 32768 | tf_op jit(solution)/shard_map/all_to_all | solution.py:341
  59.5 0.8 %shard_map.45 = (f32[8,16,128]{2,1,0:T(8,128)S(1)}, f32[32,128]{1,0:T(8,128)S(1)}, f32[8,16,128]{2,1,0:T(8,128)S(1)}, f32[8,16,128]{2,1,0:T(8,128)S(1)}) custom-call(bf16[8,1152,128]{2,1,0:T(8,128)(2,1)S(1)} %shard_map.41.refs_0_, f32[32,128]{1,0:T(8,128)S(1)} %bitcast.36, f32[8,16,128]{2,1,0:T(8,128)S(1)} %get-tuple-element.31.refs_2_, ...), custom_call_target="tpu_custom_call" | custom-call | flops 37748736 | bytes 1802240 | tf_op jit(solution)/shard_map/pallas_call | solution.py:329
  60.2 8.9 %all_to_all.47 = f32[32,1,128]{2,1,0:T(1,128)S(1)} all-to-all(f32[32,1,128]{2,1,0:T(1,128)S(1)} %bitcast.42), channel_id=1, replica_groups=mesh['grp'=2,'ta'=4,'gz'=4] {'grp','ta','gz'}, dimensions={0} | all-to-all | bytes 32768 | tf_op jit(solution)/shard_map/all_to_all | solution.py:341
  69.1 0.8 %shard_map.46 = (f32[128,128]{1,0:T(8,128)}, f32[128,128]{1,0:T(8,128)}) custom-call(f32[32,128]{1,0:T(8,128)S(1)} %bitcast.33, f32[32,128]{1,0:T(8,128)S(1)} %bitcast.35, f32[32,128]{1,0:T(8,128)S(1)} %bitcast.37, f32[32,128]{1,0:T(8,128)S(1)} %bitcast.38, f32[8,16,128]{2,1,0:T(8,128)S(1)} %get-tuple-element.37.refs_4_, f32[128,128]{1,0:T(8,128)S(1)} %bitcast.31, ...), custom_call_target="tpu_custom_call" | custom-call | flops 377487 | bytes 720896 | tf_op jit(solution)/shard_map/pallas_call | solution.py:329
  (20 shorter events, 0.1 us)
Async XLA Ops:
  0.6 11.3 %copy-start = (f32[16,1,1,8,128]{4,3,2,1,0:T(8,128)S(1)}, f32[16,1,1,8,128]{4,3,2,1,0:T(8,128)}, u32[]{:S(2)}) copy-start(f32[16,1,1,8,128]{4,3,2,1,0:T(8,128)} %param.3) | copy-start | bytes 196612
  0.6 11.1 %collective-permute-start.4 = (f32[128,128]{1,0:T(8,128)}, f32[128,128]{1,0:T(8,128)S(1)}, u32[]{:S(2)}, u32[]{:S(2)}) collective-permute-start(f32[128,128]{1,0:T(8,128)} %bitcast.24), channel_id=1, source_target_pairs={{0,3},{1,2},{2,1},{3,0},{4,7},{5,6},{6,5},{7,4},{8,11},{9,10},{10,... | collective-permute-start | bytes 196616 | tf_op jit(solution)/shard_map/ppermute | solution.py:50
  5.8 5.9 %collective-permute-start.3 = (f32[128,128]{1,0:T(8,128)}, f32[128,128]{1,0:T(8,128)S(1)}, u32[]{:S(2)}, u32[]{:S(2)}) collective-permute-start(f32[128,128]{1,0:T(8,128)} %bitcast.25), channel_id=1, source_target_pairs={{0,1},{1,0},{2,3},{3,2},{4,5},{5,4},{6,7},{7,6},{8,9},{9,8},{10,11... | collective-permute-start | bytes 196616 | tf_op jit(solution)/shard_map/ppermute | solution.py:50
  5.8 5.9 %collective-permute-start.2 = (f32[128,128]{1,0:T(8,128)}, f32[128,128]{1,0:T(8,128)S(1)}, u32[]{:S(2)}, u32[]{:S(2)}) collective-permute-start(f32[128,128]{1,0:T(8,128)} %bitcast.26), channel_id=1, source_target_pairs={{0,12},{4,8},{8,4},{12,0},{1,13},{5,9},{9,5},{13,1},{2,14},{6,10},... | collective-permute-start | bytes 196616 | tf_op jit(solution)/shard_map/ppermute | solution.py:50
  6.5 5.3 %collective-permute-start.1 = (f32[128,128]{1,0:T(8,128)}, f32[128,128]{1,0:T(8,128)S(1)}, u32[]{:S(2)}, u32[]{:S(2)}) collective-permute-start(f32[128,128]{1,0:T(8,128)} %bitcast.27), channel_id=1, source_target_pairs={{0,4},{4,0},{8,12},{12,8},{1,5},{5,1},{9,13},{13,9},{2,6},{6,2},{1... | collective-permute-start | bytes 196616 | tf_op jit(solution)/shard_map/ppermute | solution.py:50
  7.4 4.5 %collective-permute-start = (f32[128,128]{1,0:T(8,128)}, f32[128,128]{1,0:T(8,128)S(1)}, u32[]{:S(2)}, u32[]{:S(2)}) collective-permute-start(f32[128,128]{1,0:T(8,128)} %bitcast.28), channel_id=1, source_target_pairs={{16,0},{0,16},{17,1},{1,17},{18,2},{2,18},{19,3},{3,19},{20,4},{4,... | collective-permute-start | bytes 196616 | tf_op jit(solution)/shard_map/ppermute | solution.py:46
  12.6 15.4 %collective-permute-start.9 = (f32[8,16,128]{2,1,0:T(8,128)S(1)}, f32[8,16,128]{2,1,0:T(8,128)S(1)}, u32[]{:S(2)}, u32[]{:S(2)}) collective-permute-start(f32[8,16,128]{2,1,0:T(8,128)S(1)} %get-tuple-element.23.refs_2_), channel_id=1, source_target_pairs={{0,3},{1,2},{2,1},{3,0},{4,7},{5,6},{6,5},{7,4},{8,11},{9,10},{10,... | collective-permute-start | bytes 196616 | tf_op jit(solution)/shard_map/ppermute | solution.py:50
  13.5 14.5 %collective-permute-start.8 = (f32[8,16,128]{2,1,0:T(8,128)S(1)}, f32[8,16,128]{2,1,0:T(8,128)S(1)}, u32[]{:S(2)}, u32[]{:S(2)}) collective-permute-start(f32[8,16,128]{2,1,0:T(8,128)S(1)} %get-tuple-element.23.refs_2_), channel_id=1, source_target_pairs={{0,1},{1,0},{2,3},{3,2},{4,5},{5,4},{6,7},{7,6},{8,9},{9,8},{10,11... | collective-permute-start | bytes 196616 | tf_op jit(solution)/shard_map/ppermute | solution.py:50
  14.7 13.3 %collective-permute-start.7 = (f32[8,16,128]{2,1,0:T(8,128)S(1)}, f32[8,16,128]{2,1,0:T(8,128)S(1)}, u32[]{:S(2)}, u32[]{:S(2)}) collective-permute-start(f32[8,16,128]{2,1,0:T(8,128)S(1)} %get-tuple-element.23.refs_2_), channel_id=1, source_target_pairs={{0,12},{4,8},{8,4},{12,0},{1,13},{5,9},{9,5},{13,1},{2,14},{6,10},... | collective-permute-start | bytes 196616 | tf_op jit(solution)/shard_map/ppermute | solution.py:50
  14.7 13.3 %collective-permute-start.6 = (f32[8,16,128]{2,1,0:T(8,128)S(1)}, f32[8,16,128]{2,1,0:T(8,128)S(1)}, u32[]{:S(2)}, u32[]{:S(2)}) collective-permute-start(f32[8,16,128]{2,1,0:T(8,128)S(1)} %get-tuple-element.23.refs_2_), channel_id=1, source_target_pairs={{0,4},{4,0},{8,12},{12,8},{1,5},{5,1},{9,13},{13,9},{2,6},{6,2},{1... | collective-permute-start | bytes 196616 | tf_op jit(solution)/shard_map/ppermute | solution.py:50
  15.4 12.7 %collective-permute-start.5 = (f32[8,16,128]{2,1,0:T(8,128)S(1)}, f32[8,16,128]{2,1,0:T(8,128)S(1)}, u32[]{:S(2)}, u32[]{:S(2)}) collective-permute-start(f32[8,16,128]{2,1,0:T(8,128)S(1)} %get-tuple-element.23.refs_2_), channel_id=1, source_target_pairs={{16,0},{0,16},{17,1},{1,17},{18,2},{2,18},{19,3},{3,19},{20,4},{4,... | collective-permute-start | bytes 196616 | tf_op jit(solution)/shard_map/ppermute | solution.py:46
  28.8 14.9 %collective-permute-start.14 = (f32[8,16,128]{2,1,0:T(8,128)S(1)}, f32[8,16,128]{2,1,0:T(8,128)S(1)}, u32[]{:S(2)}, u32[]{:S(2)}) collective-permute-start(f32[8,16,128]{2,1,0:T(8,128)S(1)} %get-tuple-element.25.refs_2_), channel_id=1, source_target_pairs={{0,3},{1,2},{2,1},{3,0},{4,7},{5,6},{6,5},{7,4},{8,11},{9,10},{10,... | collective-permute-start | bytes 196616 | tf_op jit(solution)/shard_map/ppermute | solution.py:50
  29.5 14.2 %collective-permute-start.13 = (f32[8,16,128]{2,1,0:T(8,128)S(1)}, f32[8,16,128]{2,1,0:T(8,128)S(1)}, u32[]{:S(2)}, u32[]{:S(2)}) collective-permute-start(f32[8,16,128]{2,1,0:T(8,128)S(1)} %get-tuple-element.25.refs_2_), channel_id=1, source_target_pairs={{0,1},{1,0},{2,3},{3,2},{4,5},{5,4},{6,7},{7,6},{8,9},{9,8},{10,11... | collective-permute-start | bytes 196616 | tf_op jit(solution)/shard_map/ppermute | solution.py:50
  30.0 13.7 %collective-permute-start.12 = (f32[8,16,128]{2,1,0:T(8,128)S(1)}, f32[8,16,128]{2,1,0:T(8,128)S(1)}, u32[]{:S(2)}, u32[]{:S(2)}) collective-permute-start(f32[8,16,128]{2,1,0:T(8,128)S(1)} %get-tuple-element.25.refs_2_), channel_id=1, source_target_pairs={{0,12},{4,8},{8,4},{12,0},{1,13},{5,9},{9,5},{13,1},{2,14},{6,10},... | collective-permute-start | bytes 196616 | tf_op jit(solution)/shard_map/ppermute | solution.py:50
  30.0 13.7 %collective-permute-start.11 = (f32[8,16,128]{2,1,0:T(8,128)S(1)}, f32[8,16,128]{2,1,0:T(8,128)S(1)}, u32[]{:S(2)}, u32[]{:S(2)}) collective-permute-start(f32[8,16,128]{2,1,0:T(8,128)S(1)} %get-tuple-element.25.refs_2_), channel_id=1, source_target_pairs={{0,4},{4,0},{8,12},{12,8},{1,5},{5,1},{9,13},{13,9},{2,6},{6,2},{1... | collective-permute-start | bytes 196616 | tf_op jit(solution)/shard_map/ppermute | solution.py:50
  30.7 13.0 %collective-permute-start.10 = (f32[8,16,128]{2,1,0:T(8,128)S(1)}, f32[8,16,128]{2,1,0:T(8,128)S(1)}, u32[]{:S(2)}, u32[]{:S(2)}) collective-permute-start(f32[8,16,128]{2,1,0:T(8,128)S(1)} %get-tuple-element.25.refs_2_), channel_id=1, source_target_pairs={{16,0},{0,16},{17,1},{1,17},{18,2},{2,18},{19,3},{3,19},{20,4},{4,... | collective-permute-start | bytes 196616 | tf_op jit(solution)/shard_map/ppermute | solution.py:46
  44.6 14.9 %collective-permute-start.19 = (f32[8,16,128]{2,1,0:T(8,128)S(1)}, f32[8,16,128]{2,1,0:T(8,128)S(1)}, u32[]{:S(2)}, u32[]{:S(2)}) collective-permute-start(f32[8,16,128]{2,1,0:T(8,128)S(1)} %get-tuple-element.31.refs_2_), channel_id=1, source_target_pairs={{0,3},{1,2},{2,1},{3,0},{4,7},{5,6},{6,5},{7,4},{8,11},{9,10},{10,... | collective-permute-start | bytes 196616 | tf_op jit(solution)/shard_map/ppermute | solution.py:50
  45.2 14.2 %collective-permute-start.18 = (f32[8,16,128]{2,1,0:T(8,128)S(1)}, f32[8,16,128]{2,1,0:T(8,128)S(1)}, u32[]{:S(2)}, u32[]{:S(2)}) collective-permute-start(f32[8,16,128]{2,1,0:T(8,128)S(1)} %get-tuple-element.31.refs_2_), channel_id=1, source_target_pairs={{0,1},{1,0},{2,3},{3,2},{4,5},{5,4},{6,7},{7,6},{8,9},{9,8},{10,11... | collective-permute-start | bytes 196616 | tf_op jit(solution)/shard_map/ppermute | solution.py:50
  45.8 13.7 %collective-permute-start.17 = (f32[8,16,128]{2,1,0:T(8,128)S(1)}, f32[8,16,128]{2,1,0:T(8,128)S(1)}, u32[]{:S(2)}, u32[]{:S(2)}) collective-permute-start(f32[8,16,128]{2,1,0:T(8,128)S(1)} %get-tuple-element.31.refs_2_), channel_id=1, source_target_pairs={{0,12},{4,8},{8,4},{12,0},{1,13},{5,9},{9,5},{13,1},{2,14},{6,10},... | collective-permute-start | bytes 196616 | tf_op jit(solution)/shard_map/ppermute | solution.py:50
  45.8 13.7 %collective-permute-start.16 = (f32[8,16,128]{2,1,0:T(8,128)S(1)}, f32[8,16,128]{2,1,0:T(8,128)S(1)}, u32[]{:S(2)}, u32[]{:S(2)}) collective-permute-start(f32[8,16,128]{2,1,0:T(8,128)S(1)} %get-tuple-element.31.refs_2_), channel_id=1, source_target_pairs={{0,4},{4,0},{8,12},{12,8},{1,5},{5,1},{9,13},{13,9},{2,6},{6,2},{1... | collective-permute-start | bytes 196616 | tf_op jit(solution)/shard_map/ppermute | solution.py:50
  46.4 13.0 %collective-permute-start.15 = (f32[8,16,128]{2,1,0:T(8,128)S(1)}, f32[8,16,128]{2,1,0:T(8,128)S(1)}, u32[]{:S(2)}, u32[]{:S(2)}) collective-permute-start(f32[8,16,128]{2,1,0:T(8,128)S(1)} %get-tuple-element.31.refs_2_), channel_id=1, source_target_pairs={{16,0},{0,16},{17,1},{1,17},{18,2},{2,18},{19,3},{3,19},{20,4},{4,... | collective-permute-start | bytes 196616 | tf_op jit(solution)/shard_map/ppermute | solution.py:46
